TPU v7x, 512 devices: a whole 4x4x16 slice. The times are simulated.
512 devices in a mesh: req: 32 (over z, core), hid: 16 (over x, y).
Axes of the slice: x: 4, y: 4, z: 16, core: 2. Of those that a mesh axis runs over, the one named last changes fastest.
Arguments:
- attn_partial: bfloat16 [16, 2048, 2880], P('hid', 'req'), may hold values from -4 to 4
- residual: bfloat16 [2048, 2880], P('req'), may hold values from -6 to 6
- norm_gain: bfloat16 [2880], replicated, may hold values from 0.5 to 1.5
- router_weight: bfloat16 [2880, 32], replicated, may hold values from -0.02734375 to 0.02734375
- router_bias: float32 [32], replicated, may hold values from -2.5 to 2.5
- routes: int32 [2048, 4], P('req'), may hold values from 0 to 31, all different within a row; in each aligned block of 64 rows (0 to 63, 64 to 127, ...) at most 16 rows name the same one
- gate_up: bfloat16 [32, 2880, 5760], P('req', None, 'hid'), may hold values from -0.109375 to 0.109375
- gate_up_bias: bfloat16 [32, 5760], P('req', 'hid'), may hold values from -6 to 6
- down_weight: bfloat16 [32, 2880, 2880], P('req', 'hid'), may hold values from -0.0546875 to 0.0546875
- down_bias: bfloat16 [32, 2880], P('req'), may hold values from -6 to 6
Outputs:
- layer_out: bfloat16 [2048, 2880], P('req')
Inputs may be any that keep to these rules, and one draw needn't show every extreme that they name: `routes`: each row names 4 different experts; among the 64 rows of one request group no expert is named by more than 16 rows, and in every draw some expert is named by exactly 16 rows of some group.
All inputs are finite; a program needn't handle non-finite values.
Results may differ from a plain program's by a relative error of at most 0.022.
Values may be sent and summed in bfloat16 or wider, within the bound.
A program may use at most 64 MiB of HBM per device.

v0:
```python
import jax
import jax.numpy as jnp
from jax import lax
from jax.sharding import PartitionSpec as P


def route_tables(routes, experts, capacity):
    row_count, top_count = routes.shape
    pair_ids = routes.reshape(row_count * top_count)
    onehot = (pair_ids[:, None] == jnp.arange(experts, dtype=jnp.int32)[None, :]).astype(jnp.int32)
    before = jnp.cumsum(onehot, axis=0) - onehot
    slot_ids = jnp.sum(before * onehot, axis=1)
    return (pair_ids * capacity + slot_ids).reshape(row_count, top_count)


def placed(target, values, columns_total):
    columns = jnp.arange(columns_total, dtype=jnp.int32)
    matches = target[:, :, None] == columns[None, None, :]
    return jnp.sum(jnp.where(matches, values[:, :, None], 0.0), axis=1)


def on_device(
    attn_partial,
    residual,
    norm_gain,
    router_weight,
    router_bias,
    routes,
    gate_up,
    gate_up_bias,
    down_weight,
    down_bias,
):
    req_count = lax.axis_size("req")
    row_count, features = residual.shape
    experts = router_weight.shape[1]
    top_count = routes.shape[1]
    capacity = 2 * top_count * row_count // req_count
    gain_wide = norm_gain.astype(jnp.float32)
    attention = lax.psum(attn_partial[0].astype(jnp.float32).astype(jnp.bfloat16), "hid").astype(
        jnp.float32
    )
    stream = (residual.astype(jnp.float32) + attention).astype(jnp.bfloat16)
    widened = stream.astype(jnp.float32)
    inverse = lax.rsqrt(jnp.mean(widened * widened, axis=1, keepdims=True) + 1e-05)
    normed = (widened * inverse * gain_wide).astype(jnp.bfloat16)
    logits = jnp.dot(normed, router_weight, preferred_element_type=jnp.float32) + router_bias

    def whole_rows():
        return (normed, widened)

    picked = jnp.take_along_axis(logits, routes, axis=1)
    raised = jnp.exp(picked)
    combine = (raised / jnp.sum(raised, axis=1, keepdims=True)).astype(jnp.bfloat16)
    target = route_tables(routes, experts, capacity)
    slots_total = experts * capacity
    route_matrix = placed(target, jnp.ones(target.shape, jnp.float32), slots_total).astype(
        jnp.bfloat16
    )
    weights_up = gate_up[0]
    normed_full = whole_rows()[0]
    outgoing = jnp.dot(route_matrix.T, normed_full, preferred_element_type=jnp.float32).astype(
        jnp.bfloat16
    )
    outgoing = outgoing.reshape(experts, capacity, features)
    received = lax.all_to_all(outgoing, "req", split_axis=0, concat_axis=0, tiled=True)
    preact = jnp.dot(
        received.reshape(req_count * capacity, features),
        weights_up,
        preferred_element_type=jnp.float32,
    )
    preact = preact + gate_up_bias[0].astype(jnp.float32)
    gate_part = jnp.minimum(preact[:, 0::2], 7.0)
    up_part = jnp.clip(preact[:, 1::2], -7.0, 7.0)
    activated = ((up_part + 1.0) * gate_part * jax.nn.sigmoid(1.702 * gate_part)).astype(
        jnp.bfloat16
    )
    partial_value = jnp.dot(activated, down_weight[0], preferred_element_type=jnp.float32)
    partial_value = partial_value.astype(jnp.bfloat16).astype(jnp.float32)
    combine_matrix = placed(target, combine.astype(jnp.float32), slots_total).astype(jnp.bfloat16)
    summed = lax.psum(partial_value.astype(jnp.bfloat16), "hid").astype(jnp.float32)
    expert_out = (summed + down_bias[0].astype(jnp.float32)).astype(jnp.bfloat16)
    expert_out = expert_out.reshape(req_count, capacity, features)
    returned = lax.all_to_all(expert_out, "req", split_axis=0, concat_axis=0, tiled=True)
    mixture = jnp.dot(
        combine_matrix, returned.reshape(slots_total, features), preferred_element_type=jnp.float32
    )
    widened_full = whole_rows()[1]
    return (widened_full + mixture).astype(jnp.bfloat16)


def solution(mesh):
    return jax.shard_map(
        on_device,
        mesh=mesh,
        in_specs=(
            P("hid", "req", None),
            P("req", None),
            P(),
            P(),
            P(),
            P("req", None),
            P("req", None, "hid"),
            P("req", "hid"),
            P("req", "hid", None),
            P("req", None),
        ),
        out_specs=P("req", None),
        check_vma=False,
    )
```

profile of v0, /device:TPU:1, one launch (start us, length us, event | category | flops | bytes accessed | tf_op | source)
XLA Modules:
  0.0 591.3 jit_solution(12012518058343366653)
XLA Ops:
  6.5 0.7 all-reduce.3.cloned.1.call-update
  7.3 0.7 bitcast_or_fusion
  8.0 0.8 copy.39
  8.7 0.1 eq.49
  8.8 0.6 reduce-window.6
  9.4 0.2 slice_reduce_fusion
  9.6 0.1 eq.45
  9.7 0.7 convert_element_type.73
  10.5 0.1 reshape.77
  10.7 0.1 fusion.20
  10.8 0.1 reduce_sum.48
  11.0 0.7 multiply_add_fusion
  11.7 118.0 %all-reduce.3.cloned.1.call-done = bf16[64,2880]{1,0:T(8,128)(2,1)} async-done(((bf16[64,2880]{1,0:T(8,128)(2,1)}), bf16[64,2880]{1,0:T(8,128)(2,1)}) %all-reduce.3.cloned.1.call-update) | async-done | bytes 368656 | tf_op jit(solution)/shard_map/psum | solution.py:40
  129.7 1.3 fusion.7
  131.0 1.2 convolution_add_fusion.1
  132.3 2.0 gather_fusion
  134.3 0.1 reshape.80
  134.5 0.2 select_reduce_fusion.1
  134.7 2.7 convolution_convert_fusion.1
  137.4 4.6 copy.45
  142.0 14.5 %all-to-all-start = ((bf16[32,16,2880]{2,1,0:T(8,128)(2,1)}), bf16[32,16,2880]{2,1,0:T(8,128)(2,1)}, u32[]{:S(2)}, u32[]{:S(2)}) async-start(bf16[32,16,2880]{2,1,0:T(8,128)(2,1)} %bitcast.41), calls=%async_computation | async-start | bytes 6029312 | tf_op jit(solution)/shard_map/all_to_all | solution.py:66
  156.5 135.6 %all-to-all-done = bf16[32,16,2880]{2,1,0:T(8,128)(2,1)} async-done(((bf16[32,16,2880]{2,1,0:T(8,128)(2,1)}), bf16[32,16,2880]{2,1,0:T(8,128)(2,1)}, u32[]{:S(2)}, u32[]{:S(2)}) %all-to-all-start) | async-done | bytes 2949152 | tf_op jit(solution)/shard_map/all_to_all | solution.py:66
  292.2 3.2 fusion.3
  295.4 1.5 slice.14
  296.8 1.4 slice.15
  298.3 4.2 convolution_convert_fusion
  302.5 0.7 copy-done.2
  303.2 117.7 %all-reduce.5.cloned.1.call-done = bf16[512,2880]{0,1:T(8,128)(2,1)} async-done(((bf16[512,2880]{0,1:T(8,128)(2,1)}), bf16[512,2880]{0,1:T(8,128)(2,1)}) %all-reduce.5.cloned.1.call-update) | async-done | bytes 2949136 | tf_op jit(solution)/shard_map/psum | solution.py:81
  420.9 4.1 add_convert_fusion
  425.0 4.6 copy.46
  429.5 153.5 %all_to_all.10 = bf16[32,16,2880]{2,1,0:T(8,128)(2,1)S(1)} all-to-all(bf16[32,16,2880]{2,1,0:T(8,128)(2,1)} %bitcast.42), channel_id=1, replica_groups=mesh['req'=32,'hid'=16] {'req'}, dimensions={0} | all-to-all | bytes 5898240 | tf_op jit(solution)/shard_map/all_to_all | solution.py:84
  583.0 1.4 fusion
  (21 shorter events, 0.5 us)
Async XLA Ops:
  6.5 285.6 %copy-start = (bf16[1,2880,360]{1,2,0:T(8,128)(2,1)S(1)}, bf16[1,2880,360]{1,2,0:T(8,128)(2,1)}, u32[]{:S(2)}) copy-start(bf16[1,2880,360]{1,2,0:T(8,128)(2,1)} %param.16) | copy-start | bytes 6220804
  6.5 123.1 %all-reduce.3.cloned.1.call-start = ((), (), s32[]{:S(2)}) async-start(), calls=%async_computation.2 | async-start | bytes 753664 | tf_op jit(solution)/shard_map/psum | solution.py:40
  132.3 2.2 copy-start.1
  142.0 14.5 %copy-start.3 = (bf16[1,360]{1,0:T(2,128)(2,1)S(1)}, bf16[1,360]{1,0:T(2,128)(2,1)}, u32[]{:S(2)}) copy-start(bf16[1,360]{1,0:T(2,128)(2,1)} %param.17) | copy-start | bytes 2164
  142.0 150.2 %all-to-all-start = ((bf16[32,16,2880]{2,1,0:T(8,128)(2,1)}), bf16[32,16,2880]{2,1,0:T(8,128)(2,1)}, u32[]{:S(2)}, u32[]{:S(2)}) async-start(bf16[32,16,2880]{2,1,0:T(8,128)(2,1)} %bitcast.41), calls=%async_computation | async-start | bytes 6029312 | tf_op jit(solution)/shard_map/all_to_all | solution.py:66
  156.4 264.5 %all-reduce.5.cloned.1.call-start = ((), (), s32[]{:S(2)}) async-start(), calls=%async_computation.3 | async-start | bytes 5898240 | tf_op jit(solution)/shard_map/psum | solution.py:81
  302.5 0.7 copy-start.2
Sparse Core Ops, SparseCore 0:
  10.6 119.0 all-reduce.2
  302.6 118.2 all-reduce.4
where the time goes:
time: 592 us; the launch traced here: 591 us
  waiting for transfers between devices  372 us (63%)
  blocking collectives  154 us (26%)
  local copies, waits for them, and re-layouts  16.5 us (3%)
  starting transfers between devices  14.5 us (2%)
  between operations  13.5 us (2%)
  matrix products  12.7 us (2%)
  other arithmetic  8.49 us (1%)
    all_to_all x1, blocking collectives, on_device(): lax.all_to_all(expert_out, 'req', split_axis=0, concat_axis=0, tiled=True)  154 us
    all_to_all x1, waiting for transfers between devices, on_device(): lax.all_to_all(outgoing, 'req', split_axis=0, concat_axis=0, tiled=True)  136 us
    psum x1, waiting for transfers between devices, on_device(): lax.psum(attn_partial[0].astype(jnp.float32).astype(jnp.bfloat16), 'hid')  118 us
    psum x1, waiting for transfers between devices, on_device(): lax.psum(partial_value.astype(jnp.bfloat16), 'hid').astype(jnp.float32)  118 us
    all_to_all x1, starting transfers between devices, on_device(): lax.all_to_all(outgoing, 'req', split_axis=0, concat_axis=0, tiled=True)  14.5 us
  transfers between devices with their start and end apart: 3, of which 3 were waited for; matrix products, arithmetic and copies ran while one was open for 1% of the time, Pallas kernels for 0%

commit v1 on v0

v1 whole, which is shorter than its diff:
```python
import functools

import jax
import jax.numpy as jnp
from jax import lax
from jax.experimental import pallas as pl
from jax.experimental.pallas import tpu as pltpu
from jax.sharding import PartitionSpec as P

MESH = pl.DeviceIdType.MESH
BLK = 384
NBLK = 8
SLOTS = 8
BF = jnp.bfloat16
F32 = jnp.float32


def lanes(block):
    return pl.ds(pl.multiple_of(block * BLK, 128), BLK)


def moe_kernel(
    n_req,
    n_hid,
    attn_ref,
    resid_ref,
    gain_ref,
    wr_ref,
    rb_ref,
    routes_ref,
    bgu_ref,
    db_ref,
    wgu_hbm,
    wd_hbm,
    out_ref,
    attn_s,
    resid_s,
    gain_s,
    wr_s,
    db_s,
    wgu_v,
    wd_v,
    wg_s,
    wd_s,
    r1,
    stat_s,
    rstat,
    zout,
    zin,
    ag,
    acc,
    ssq,
    act_s,
    pout,
    rs,
    zbout,
    zbin,
    fin_s,
    rfin,
    w_sem,
    s1,
    q1,
    s2,
    q2,
    s3,
    q3,
    s4,
    q4,
    s5,
    q5,
    s6,
    q6,
    s7,
    q7,
):
    rows, width = attn_ref.shape
    experts = rb_ref.shape[1]
    half = wd_hbm.shape[0]
    wide = BLK * NBLK
    tail = wide - 256
    h = lax.axis_index("hid")
    g = lax.axis_index("req")
    sg = lax.div(h, NBLK)
    f = lax.rem(h, NBLK)

    get_wgu = pltpu.make_async_copy(wgu_hbm, wgu_v, w_sem.at[0])
    get_wd = pltpu.make_async_copy(wd_hbm, wd_v, w_sem.at[1])
    get_wgu.start()
    get_wd.start()

    barrier = pltpu.get_barrier_semaphore()

    @pl.loop(1, n_hid)
    def _(d):
        pl.semaphore_signal(
            barrier, inc=1, device_id={"hid": lax.rem(h + d, n_hid)}, device_id_type=MESH
        )

    @pl.loop(1, n_req)
    def _(d):
        pl.semaphore_signal(
            barrier, inc=1, device_id={"req": lax.rem(g + d, n_req)}, device_id_type=MESH
        )

    attn_s[:, tail:] = jnp.zeros((rows, wide - tail), BF)
    attn_s[:, :width] = attn_ref[...]
    resid_s[:, tail:] = jnp.zeros((rows, wide - tail), BF)
    resid_s[:, :width] = resid_ref[...]
    gain_s[:, tail:] = jnp.zeros((1, wide - tail), F32)
    gain_s[:, :width] = gain_ref[...].astype(F32)
    db_s[:, tail:] = jnp.zeros((1, wide - tail), F32)
    db_s[:, :width] = db_ref[...].astype(F32)

    pl.semaphore_wait(barrier, n_hid + n_req - 2)

    def hid_copy(src, dst, send, recv, peer):
        return pltpu.make_async_remote_copy(
            src_ref=src,
            dst_ref=dst,
            send_sem=send,
            recv_sem=recv,
            device_id={"hid": peer},
            device_id_type=MESH,
        )

    def req_copy(src, dst, send, recv, peer):
        return pltpu.make_async_remote_copy(
            src_ref=src,
            dst_ref=dst,
            send_sem=send,
            recv_sem=recv,
            device_id={"req": peer},
            device_id_type=MESH,
        )

    @pl.loop(1, n_hid)
    def _(d):
        p = lax.rem(h + d, n_hid)
        src = attn_s.at[:, lanes(lax.rem(p, NBLK))]
        hid_copy(src, r1.at[h], s1.at[p], q1.at[h], p).start()

    wr_s[pl.ds(width, wide - width), :] = jnp.zeros((wide - width, 128), BF)
    spread = (
        lax.broadcasted_iota(jnp.int32, (experts, 128), 0)
        == lax.broadcasted_iota(jnp.int32, (experts, 128), 1)
    ).astype(BF)
    wr_s[pl.ds(0, width), :] = jnp.dot(
        wr_ref[...], spread, preferred_element_type=F32
    ).astype(BF)
    named = lax.broadcasted_iota(jnp.int32, (rows, experts), 1)
    mask = jnp.zeros((rows, experts), F32)
    for k in range(routes_ref.shape[1]):
        mask = mask + jnp.where(routes_ref[:, k : k + 1] == named, 1.0, 0.0)
    earlier = (
        lax.broadcasted_iota(jnp.int32, (rows, rows), 1)
        < lax.broadcasted_iota(jnp.int32, (rows, rows), 0)
    ).astype(BF)
    slot = jnp.dot(earlier, mask.astype(BF), preferred_element_type=F32)
    pairs = experts * SLOTS
    col = lax.broadcasted_iota(jnp.int32, (experts, pairs), 1)
    own = lax.broadcasted_iota(jnp.int32, (experts, pairs), 0)
    expand = (lax.div(col, SLOTS) == own).astype(BF)
    slot_wide = jnp.dot(slot.astype(BF), expand, preferred_element_type=F32)
    mask_wide = jnp.dot(mask.astype(BF), expand, preferred_element_type=F32)
    want = lax.rem(lax.broadcasted_iota(jnp.int32, (rows, pairs), 1), SLOTS) + sg * SLOTS
    chosen = jnp.where((slot_wide == want.astype(F32)) & (mask_wide > 0.5), 1.0, 0.0)

    def add1(d, total):
        p = lax.rem(h - d + n_hid, n_hid)
        hid_copy(r1.at[p], r1.at[p], s1.at[p], q1.at[p], p).wait_recv()
        return total + r1[p].astype(F32)

    attention = lax.fori_loop(1, n_hid, add1, attn_s[:, lanes(f)].astype(F32))
    stream = (resid_s[:, lanes(f)].astype(F32) + attention).astype(BF)
    stream_wide = stream.astype(F32)

    picked = lax.dot_general(
        chosen.astype(BF), stream, (((0,), (0,)), ((), ())), preferred_element_type=F32
    )
    zout[...] = picked.reshape(experts, SLOTS, BLK).astype(BF)

    @pl.loop(1, n_req)
    def _(d):
        p = lax.rem(g + d, n_req)
        req_copy(zout.at[p], zin.at[g], s2.at[p], q2.at[g], p).start()

    scaled = (stream_wide * gain_s[:, lanes(f)]).astype(BF)
    stats = jnp.dot(
        scaled, wr_s[pl.ds(pl.multiple_of(f * BLK, 128), BLK), :], preferred_element_type=F32
    )
    squares = jnp.sum(stream_wide * stream_wide, axis=1, keepdims=True)
    lane = lax.broadcasted_iota(jnp.int32, (rows, 128), 1)
    stat_s[...] = jnp.where(lane == experts, squares, stats)

    @pl.loop(1, NBLK)
    def _(d):
        pf = lax.rem(f + d, NBLK)
        hid_copy(
            stat_s, rstat.at[f], s3.at[pf], q3.at[f], sg * NBLK + pf
        ).start()

    get_wgu.wait()
    twice = wgu_v.shape[1]
    from_col = lax.broadcasted_iota(jnp.int32, (twice, 512), 0)
    to_col = lax.broadcasted_iota(jnp.int32, (twice, 512), 1)
    perm = (to_col == lax.rem(from_col, 2) * 256 + lax.div(from_col, 2)).astype(BF)

    @pl.loop(0, width // 192)
    def _(i):
        at = pl.ds(pl.multiple_of(i * 192, 64), 192)
        wg_s[at, :] = jnp.dot(wgu_v[at, :], perm, preferred_element_type=F32).astype(BF)

    wg_s[pl.ds(width, wide - width), :] = jnp.zeros((wide - width, 512), BF)
    bias = jnp.dot(
        jnp.broadcast_to(bgu_ref[...], (16, twice)), perm, preferred_element_type=F32
    )[0:1, :]
    get_wd.wait()
    wd_s[...] = jnp.zeros(wd_s.shape, BF)
    wd_s[0:half, 0:width] = wd_v[...]
    acc[...] = jnp.zeros(acc.shape, F32)
    ssq[...] = jnp.zeros(ssq.shape, F32)

    zin[g] = zout[g]

    @pl.loop(1, n_req)
    def _(d):
        p = lax.rem(g - d + n_req, n_req)
        req_copy(zin.at[p], zin.at[p], s2.at[p], q2.at[p], p).wait_recv()

    @pl.loop(1, n_hid)
    def _(d):
        p = lax.rem(h + d, n_hid)
        hid_copy(zin, ag.at[h], s4.at[p], q4.at[h], p).start()

    def use_block(block, at):
        wide_rows = block.astype(F32).reshape(n_req * SLOTS, BLK)
        side = lax.div(at, NBLK)
        blk = lax.rem(at, NBLK)
        sq = wide_rows * wide_rows
        ssq[side] += sq[:, 0:128] + sq[:, 128:256] + sq[:, 256:384]
        u = (wide_rows * gain_s[:, lanes(blk)]).astype(BF)
        w = wg_s[pl.ds(pl.multiple_of(blk * BLK, 128), BLK), :]
        acc[side] += jnp.dot(u, w, preferred_element_type=F32)

    use_block(zin[...], h)

    @pl.loop(1, n_hid)
    def _(d):
        p = lax.rem(h - d + n_hid, n_hid)
        hid_copy(ag.at[p], ag.at[p], s4.at[p], q4.at[p], p).wait_recv()
        use_block(ag[p], p)

    for side in range(2):
        mean = jnp.sum(ssq[side], axis=1, keepdims=True) * (1.0 / width)
        inverse = lax.rsqrt(mean + 1e-05)
        gate = jnp.minimum(acc[side, :, 0:256] * inverse + bias[:, 0:256], 7.0)
        up = jnp.clip(acc[side, :, 256:512] * inverse + bias[:, 256:512], -7.0, 7.0)
        act_s[side] = ((up + 1.0) * gate * jax.nn.sigmoid(1.702 * gate)).astype(BF)

    def down(p):
        return jnp.dot(
            act_s[lax.div(p, NBLK)], wd_s[:, lanes(lax.rem(p, NBLK))], preferred_element_type=F32
        ).astype(BF)

    @pl.loop(1, n_hid)
    def _(d):
        p = lax.rem(h + d, n_hid)
        pout[p] = down(p)
        hid_copy(pout.at[p], rs.at[h], s5.at[p], q5.at[h], p).start()

    total_stats = stat_s[...]
    for d in range(1, NBLK):
        pf = lax.rem(f - d + NBLK, NBLK)
        hid_copy(rstat.at[pf], rstat.at[pf], s3.at[pf], q3.at[pf], sg * NBLK + pf).wait_recv()
        total_stats = total_stats + rstat[pf]
    row_sq = jnp.sum(jnp.where(lane == experts, total_stats, 0.0), axis=1, keepdims=True)
    row_inverse = lax.rsqrt(row_sq * (1.0 / width) + 1e-05)
    logits = total_stats[:, 0:experts] * row_inverse + rb_ref[...]
    raised = jnp.where(mask > 0.5, jnp.exp(jnp.where(mask > 0.5, logits, 0.0)), 0.0)
    combine = (raised / jnp.sum(raised, axis=1, keepdims=True)).astype(BF)
    combine_wide = jnp.dot(combine, expand, preferred_element_type=F32)
    weights = jnp.where(chosen > 0.5, combine_wide, 0.0).astype(BF)

    def add5(d, total):
        p = lax.rem(h - d + n_hid, n_hid)
        hid_copy(rs.at[p], rs.at[p], s5.at[p], q5.at[p], p).wait_recv()
        return total + rs[p].astype(F32)

    summed = lax.fori_loop(1, n_hid, add5, down(h).astype(F32))
    expert_out = summed + db_s[:, lanes(f)]

    zbout[...] = expert_out.reshape(n_req, SLOTS, BLK).astype(BF)

    @pl.loop(1, n_req)
    def _(d):
        p = lax.rem(g + d, n_req)
        req_copy(zbout.at[p], zbin.at[g], s6.at[p], q6.at[g], p).start()

    zbin[g] = zbout[g]

    @pl.loop(1, n_req)
    def _(d):
        p = lax.rem(g - d + n_req, n_req)
        req_copy(zbin.at[p], zbin.at[p], s6.at[p], q6.at[p], p).wait_recv()

    returned = zbin[...].astype(F32).reshape(pairs, BLK).astype(BF)
    mixture = jnp.dot(weights, returned, preferred_element_type=F32)
    first = jnp.where(sg == 0, 1.0, 0.0)
    fin_s[...] = (mixture + stream_wide * first).astype(BF)

    @pl.loop(1, n_hid)
    def _(d):
        p = lax.rem(h + d, n_hid)
        hid_copy(fin_s, rfin.at[h], s7.at[p], q7.at[h], p).start()

    rfin[h] = fin_s[...]

    @pl.loop(1, n_hid)
    def _(d):
        p = lax.rem(h - d + n_hid, n_hid)
        hid_copy(rfin.at[p], rfin.at[p], s7.at[p], q7.at[p], p).wait_recv()

    for b in range(NBLK):
        size = min(BLK, width - b * BLK)
        both = rfin[b].astype(F32) + rfin[NBLK + b].astype(F32)
        out_ref[:, b * BLK : b * BLK + size] = both[:, :size].astype(BF)

    @pl.loop(1, n_hid)
    def _(d):
        p = lax.rem(h + d, n_hid)
        hid_copy(r1.at[p], r1.at[p], s1.at[p], q1.at[p], p).wait_send()
        hid_copy(zin, ag.at[p], s4.at[p], q4.at[p], p).wait_send()
        hid_copy(rs.at[p], rs.at[p], s5.at[p], q5.at[p], p).wait_send()
        hid_copy(fin_s, rfin.at[p], s7.at[p], q7.at[p], p).wait_send()

    @pl.loop(1, NBLK)
    def _(d):
        pf = lax.rem(f + d, NBLK)
        hid_copy(stat_s, rstat.at[pf], s3.at[pf], q3.at[pf], sg * NBLK + pf).wait_send()

    @pl.loop(1, n_req)
    def _(d):
        p = lax.rem(g + d, n_req)
        req_copy(zout.at[p], zin.at[p], s2.at[p], q2.at[p], p).wait_send()
        req_copy(zbout.at[p], zbin.at[p], s6.at[p], q6.at[p], p).wait_send()


def on_device(
    attn_partial,
    residual,
    norm_gain,
    router_weight,
    router_bias,
    routes,
    gate_up,
    gate_up_bias,
    down_weight,
    down_bias,
):
    n_req, n_hid = lax.axis_size("req"), lax.axis_size("hid")
    rows, width = residual.shape
    wide = BLK * NBLK
    per = n_req * SLOTS
    vmem = pl.BlockSpec(memory_space=pltpu.VMEM)
    hbm = pl.BlockSpec(memory_space=pl.ANY)
    dma = pltpu.SemaphoreType.DMA
    hid_sem, req_sem = dma((n_hid,)), dma((n_req,))
    return pl.pallas_call(
        functools.partial(moe_kernel, n_req, n_hid),
        out_shape=jax.ShapeDtypeStruct((rows, width), BF),
        in_specs=[vmem] * 8 + [hbm] * 2,
        out_specs=vmem,
        scratch_shapes=[
            pltpu.VMEM((rows, wide), BF),
            pltpu.VMEM((rows, wide), BF),
            pltpu.VMEM((1, wide), F32),
            pltpu.VMEM((wide, 128), BF),
            pltpu.VMEM((1, wide), F32),
            pltpu.VMEM(gate_up.shape[1:], BF),
            pltpu.VMEM(down_weight.shape[1:], BF),
            pltpu.VMEM((wide, 512), BF),
            pltpu.VMEM((256, wide), BF),
            pltpu.VMEM((n_hid, rows, BLK), BF),
            pltpu.VMEM((rows, 128), F32),
            pltpu.VMEM((NBLK, rows, 128), F32),
            pltpu.VMEM((n_req, SLOTS, BLK), BF),
            pltpu.VMEM((n_req, SLOTS, BLK), BF),
            pltpu.VMEM((n_hid, n_req, SLOTS, BLK), BF),
            pltpu.VMEM((2, per, 512), F32),
            pltpu.VMEM((2, per, 128), F32),
            pltpu.VMEM((2, per, 256), BF),
            pltpu.VMEM((n_hid, per, BLK), BF),
            pltpu.VMEM((n_hid, per, BLK), BF),
            pltpu.VMEM((n_req, SLOTS, BLK), BF),
            pltpu.VMEM((n_req, SLOTS, BLK), BF),
            pltpu.VMEM((rows, BLK), BF),
            pltpu.VMEM((n_hid, rows, BLK), BF),
            dma((2,)),
            hid_sem,
            hid_sem,
            req_sem,
            req_sem,
            dma((NBLK,)),
            dma((NBLK,)),
            hid_sem,
            hid_sem,
            hid_sem,
            hid_sem,
            req_sem,
            req_sem,
            hid_sem,
            hid_sem,
        ],
        compiler_params=pltpu.CompilerParams(
            collective_id=0, has_side_effects=True, vmem_limit_bytes=56 * 1024 * 1024
        ),
        name="moe_block",
    )(
        attn_partial[0],
        residual,
        norm_gain.reshape(1, width),
        router_weight,
        router_bias.reshape(1, -1),
        routes,
        gate_up_bias,
        down_bias,
        gate_up[0],
        down_weight[0],
    )


def solution(mesh):
    return jax.shard_map(
        on_device,
        mesh=mesh,
        in_specs=(
            P("hid", "req", None),
            P("req", None),
            P(),
            P(),
            P(),
            P("req", None),
            P("req", None, "hid"),
            P("req", "hid"),
            P("req", "hid", None),
            P("req", None),
        ),
        out_specs=P("req", None),
        check_vma=False,
    )
```

time: 592 us -> 203 us (0.34)
  waiting for transfers between devices: 372 us -> 0 us
  Pallas kernels: 0 us -> 189 us
  blocking collectives: 154 us -> 0 us
  starting transfers between devices: 14.5 us -> 0 us
  between operations: 13.5 us -> 0.01 us
  matrix products: 12.7 us -> 0 us
  other arithmetic: 8.49 us -> 0 us
    psum x2 -> x0, waiting for transfers between devices: 236 us -> none  [the longest x1 118 us: on_device(): lax.psum(attn_partial[0].astype(jnp.float32).astype(jnp.bfloat16), 'hid')]
    pallas_call x0 -> x1, Pallas kernels: none -> 189 us  [on_device(): pl.pallas_call(functools.partial(moe_kernel, n_req, n_hid), out_shape=jax...]
    all_to_all x1 -> x0, blocking collectives: 154 us -> none  [on_device(): lax.all_to_all(expert_out, 'req', split_axis=0, concat_axis=0, tiled=True)]
    all_to_all x1 -> x0, waiting for transfers between devices: 136 us -> none  [on_device(): lax.all_to_all(outgoing, 'req', split_axis=0, concat_axis=0, tiled=True)]
    all_to_all x1 -> x0, starting transfers between devices: 14.5 us -> none  [on_device(): lax.all_to_all(outgoing, 'req', split_axis=0, concat_axis=0, tiled=True)]
    dot_general x5 -> x0, matrix products: 12.7 us -> none  [the longest x1 4.19 us: on_device(): jnp.dot(activated, down_weight[0], preferred_element_type=jnp.float32)]
    convert_element_type x2 -> x0, local copies, waits for them, and re-layouts: 9.13 us -> none  [the longest x1 4.56 us: on_device(): jnp.dot(route_matrix.T, normed_full, preferred_element_type=jnp.float32)]
    unnamed x9 -> x4, local copies, waits for them, and re-layouts: 1.47 us -> 9.33 us
  transfers between devices with their start and end apart: 3 -> 0, of which waited for: 3 -> 0; matrix products, arithmetic and copies ran while one was open for 1% -> 0% of each run, Pallas kernels for 0% -> 0%
where the time goes in v1:
time: 203 us; the launch traced here: 200 us
  Pallas kernels  189 us (93%)
  local copies, waits for them, and re-layouts  10.6 us (5%)
    pallas_call x1, Pallas kernels, on_device(): pl.pallas_call(functools.partial(moe_kernel, n_req, n_hid), out_shape=jax...  189 us
    unnamed x4, local copies, waits for them, and re-layouts  9.33 us

profile of v1, /device:TPU:1, one launch (start us, length us, event | category | flops | bytes accessed | tf_op | source)
XLA Modules:
  0.0 199.9 jit_solution(18365671820211958630)
XLA Ops:
  0.0 1.3 reshape.6.gain_ref
  1.3 1.4 copy.13.routes_ref
  2.7 2.1 %copy.12.wr_ref = bf16[2880,32]{1,0:T(8,128)(2,1)} copy(bf16[2880,32]{0,1:T(8,128)(2,1)} %param.13) | data formatting | bytes 368640 | tf_op args[3]
  4.8 4.1 %copy.11 = bf16[1,2880,360]{2,1,0:T(8,128)(2,1)} copy(bf16[1,2880,360]{1,2,0:T(8,128)(2,1)} %param.16) | data formatting | bytes 4147200 | tf_op args[6]
  8.9 189.2 %moe_block.1 = bf16[64,2880]{1,0:T(8,128)(2,1)} custom-call(bf16[64,2880]{1,0:T(8,128)(2,1)} %bitcast.6, bf16[64,2880]{1,0:T(8,128)(2,1)} %resid_ref.1, bf16[1,2880]{1,0:T(2,128)(2,1)} %reshape.6.gain_ref, bf16[2880,32]{1,0:T(8,128)(2,1)} %copy.12.wr_ref, f32[1,32]{1,0:T(1,128)} %bitcast.7, s32[64,4]{1,0:T(8,128)} %copy.13.routes_ref, ...), custom_call_target="tpu_custom_call" | custom-call | tf_op jit(solution)/shard_map/moe_block/pallas_call | solution.py:368
  198.1 1.8 copy.15

commit v2 on v1

--- a/solution.py
+++ b/solution.py
@@ -17,6 +17,12 @@
 
 def lanes(block):
     return pl.ds(pl.multiple_of(block * BLK, 128), BLK)
+
+
+def dot_nt(left, right):
+    return lax.dot_general(
+        left, right, (((1,), (1,)), ((), ())), preferred_element_type=F32
+    )
 
 
 def moe_kernel(
@@ -46,13 +52,16 @@
     stat_s,
     rstat,
     zout,
-    zin,
     ag,
     acc,
     ssq,
     act_s,
     pout,
-    rs,
+    tot,
+    rb1,
+    rb2,
+    ra1,
+    ra2,
     zbout,
     zbin,
     fin_s,
@@ -139,31 +148,28 @@
         src = attn_s.at[:, lanes(lax.rem(p, NBLK))]
         hid_copy(src, r1.at[h], s1.at[p], q1.at[h], p).start()
 
-    wr_s[pl.ds(width, wide - width), :] = jnp.zeros((wide - width, 128), BF)
-    spread = (
-        lax.broadcasted_iota(jnp.int32, (experts, 128), 0)
-        == lax.broadcasted_iota(jnp.int32, (experts, 128), 1)
-    ).astype(BF)
-    wr_s[pl.ds(0, width), :] = jnp.dot(
-        wr_ref[...], spread, preferred_element_type=F32
-    ).astype(BF)
-    named = lax.broadcasted_iota(jnp.int32, (rows, experts), 1)
-    mask = jnp.zeros((rows, experts), F32)
-    for k in range(routes_ref.shape[1]):
-        mask = mask + jnp.where(routes_ref[:, k : k + 1] == named, 1.0, 0.0)
-    earlier = (
-        lax.broadcasted_iota(jnp.int32, (rows, rows), 1)
-        < lax.broadcasted_iota(jnp.int32, (rows, rows), 0)
-    ).astype(BF)
-    slot = jnp.dot(earlier, mask.astype(BF), preferred_element_type=F32)
+    wr_s[...] = jnp.zeros(wr_s.shape, BF)
+    wr_s[0:experts, 0:width] = wr_ref[...]
+    named = lax.broadcasted_iota(jnp.int32, (experts, rows), 0)
+    mask_t = jnp.zeros((experts, rows), F32)
+    for k in range(routes_ref.shape[0]):
+        mask_t = mask_t + jnp.where(routes_ref[k : k + 1, :] == named, 1.0, 0.0)
+    row_a = lax.broadcasted_iota(jnp.int32, (rows, rows), 0)
+    row_b = lax.broadcasted_iota(jnp.int32, (rows, rows), 1)
+    same = (row_a == row_b).astype(BF)
+    mask_t = mask_t.astype(BF)
+    slot_t = jnp.dot(mask_t, (row_a < row_b).astype(BF), preferred_element_type=F32)
     pairs = experts * SLOTS
-    col = lax.broadcasted_iota(jnp.int32, (experts, pairs), 1)
-    own = lax.broadcasted_iota(jnp.int32, (experts, pairs), 0)
-    expand = (lax.div(col, SLOTS) == own).astype(BF)
-    slot_wide = jnp.dot(slot.astype(BF), expand, preferred_element_type=F32)
-    mask_wide = jnp.dot(mask.astype(BF), expand, preferred_element_type=F32)
-    want = lax.rem(lax.broadcasted_iota(jnp.int32, (rows, pairs), 1), SLOTS) + sg * SLOTS
-    chosen = jnp.where((slot_wide == want.astype(F32)) & (mask_wide > 0.5), 1.0, 0.0)
+    col = lax.broadcasted_iota(jnp.int32, (pairs, experts), 0)
+    own = lax.broadcasted_iota(jnp.int32, (pairs, experts), 1)
+    expand_t = (lax.div(col, SLOTS) == own).astype(BF)
+    slot_wide = jnp.dot(expand_t, slot_t.astype(BF), preferred_element_type=F32)
+    mask_wide = jnp.dot(expand_t, mask_t, preferred_element_type=F32)
+    want = lax.rem(lax.broadcasted_iota(jnp.int32, (pairs, rows), 0), SLOTS) + sg * SLOTS
+    chosen_t = jnp.where((slot_wide == want.astype(F32)) & (mask_wide > 0.5), 1.0, 0.0)
+    chosen_t = chosen_t.astype(BF)
+    chosen = dot_nt(same, chosen_t)
+    mask = dot_nt(same, mask_t)
 
     def add1(d, total):
         p = lax.rem(h - d + n_hid, n_hid)
@@ -174,20 +180,16 @@
     stream = (resid_s[:, lanes(f)].astype(F32) + attention).astype(BF)
     stream_wide = stream.astype(F32)
 
-    picked = lax.dot_general(
-        chosen.astype(BF), stream, (((0,), (0,)), ((), ())), preferred_element_type=F32
-    )
+    picked = jnp.dot(chosen_t, stream, preferred_element_type=F32)
     zout[...] = picked.reshape(experts, SLOTS, BLK).astype(BF)
 
     @pl.loop(1, n_req)
     def _(d):
         p = lax.rem(g + d, n_req)
-        req_copy(zout.at[p], zin.at[g], s2.at[p], q2.at[g], p).start()
+        req_copy(zout.at[p], ag.at[h, g], s2.at[p], q2.at[g], p).start()
 
     scaled = (stream_wide * gain_s[:, lanes(f)]).astype(BF)
-    stats = jnp.dot(
-        scaled, wr_s[pl.ds(pl.multiple_of(f * BLK, 128), BLK), :], preferred_element_type=F32
-    )
+    stats = dot_nt(scaled, wr_s[:, lanes(f)])
     squares = jnp.sum(stream_wide * stream_wide, axis=1, keepdims=True)
     lane = lax.broadcasted_iota(jnp.int32, (rows, 128), 1)
     stat_s[...] = jnp.where(lane == experts, squares, stats)
@@ -200,73 +202,216 @@
         ).start()
 
     get_wgu.wait()
-    twice = wgu_v.shape[1]
-    from_col = lax.broadcasted_iota(jnp.int32, (twice, 512), 0)
-    to_col = lax.broadcasted_iota(jnp.int32, (twice, 512), 1)
+    twice = wgu_v.shape[0]
+    from_col = lax.broadcasted_iota(jnp.int32, (512, twice), 1)
+    to_col = lax.broadcasted_iota(jnp.int32, (512, twice), 0)
     perm = (to_col == lax.rem(from_col, 2) * 256 + lax.div(from_col, 2)).astype(BF)
-
-    @pl.loop(0, width // 192)
+    wg_s[:, tail:] = jnp.zeros((512, wide - tail), BF)
+
+    @pl.loop(0, width // BLK)
     def _(i):
-        at = pl.ds(pl.multiple_of(i * 192, 64), 192)
-        wg_s[at, :] = jnp.dot(wgu_v[at, :], perm, preferred_element_type=F32).astype(BF)
-
-    wg_s[pl.ds(width, wide - width), :] = jnp.zeros((wide - width, 512), BF)
-    bias = jnp.dot(
-        jnp.broadcast_to(bgu_ref[...], (16, twice)), perm, preferred_element_type=F32
-    )[0:1, :]
+        at = lanes(i)
+        wg_s[:, at] = jnp.dot(perm, wgu_v[:, at], preferred_element_type=F32).astype(BF)
+
+    last = width // BLK * BLK
+    wg_s[:, last:width] = jnp.dot(
+        perm, wgu_v[:, last:width], preferred_element_type=F32
+    ).astype(BF)
+    bias = dot_nt(jnp.broadcast_to(bgu_ref[...], (16, twice)), perm)[0:1, :]
     get_wd.wait()
     wd_s[...] = jnp.zeros(wd_s.shape, BF)
     wd_s[0:half, 0:width] = wd_v[...]
     acc[...] = jnp.zeros(acc.shape, F32)
     ssq[...] = jnp.zeros(ssq.shape, F32)
 
-    zin[g] = zout[g]
-
-    @pl.loop(1, n_req)
-    def _(d):
-        p = lax.rem(g - d + n_req, n_req)
-        req_copy(zin.at[p], zin.at[p], s2.at[p], q2.at[p], p).wait_recv()
-
-    @pl.loop(1, n_hid)
-    def _(d):
-        p = lax.rem(h + d, n_hid)
-        hid_copy(zin, ag.at[h], s4.at[p], q4.at[h], p).start()
-
-    def use_block(block, at):
-        wide_rows = block.astype(F32).reshape(n_req * SLOTS, BLK)
-        side = lax.div(at, NBLK)
-        blk = lax.rem(at, NBLK)
+    side = 4
+    x = lax.div(h, side)
+    y = lax.rem(h, side)
+
+    def at(c, da, db):
+        a = lax.rem((x if c == 0 else y) + da, side)
+        b = lax.rem((y if c == 0 else x) + db, side)
+        return a * side + b if c == 0 else b * side + a
+
+    quart = n_req // 4
+
+    def piece(p, q):
+        return ag.at[p, pl.ds(q * quart, quart)]
+
+    def ship(q, k, p, peer):
+        hid_copy(piece(p, q), piece(p, q), s4.at[q, k], q4.at[p, q], peer).start()
+
+    def arrive(q, p):
+        hid_copy(piece(p, q), piece(p, q), s4.at[q, 0], q4.at[p, q], p).wait_recv()
+
+    def use_half(p, c):
+        wide_rows = ag[p, c * 2 * quart : (c + 1) * 2 * quart].astype(F32)
+        count = 2 * quart * SLOTS
+        wide_rows = wide_rows.reshape(count, BLK)
+        to = lax.div(p, NBLK)
+        blk = lax.rem(p, NBLK)
         sq = wide_rows * wide_rows
-        ssq[side] += sq[:, 0:128] + sq[:, 128:256] + sq[:, 256:384]
+        here = slice(c * count, (c + 1) * count)
+        ssq[to, here] += sq[:, 0:128] + sq[:, 128:256] + sq[:, 256:384]
         u = (wide_rows * gain_s[:, lanes(blk)]).astype(BF)
-        w = wg_s[pl.ds(pl.multiple_of(blk * BLK, 128), BLK), :]
-        acc[side] += jnp.dot(u, w, preferred_element_type=F32)
-
-    use_block(zin[...], h)
-
-    @pl.loop(1, n_hid)
-    def _(d):
-        p = lax.rem(h - d + n_hid, n_hid)
-        hid_copy(ag.at[p], ag.at[p], s4.at[p], q4.at[p], p).wait_recv()
-        use_block(ag[p], p)
-
-    for side in range(2):
-        mean = jnp.sum(ssq[side], axis=1, keepdims=True) * (1.0 / width)
+        acc[to, here] += dot_nt(u, wg_s[:, lanes(blk)])
+
+    ag[h, g] = zout[g]
+    for q in range(4):
+        c = q // 2
+
+        @pl.loop(q * quart, (q + 1) * quart)
+        def _(p):
+            @pl.when(p != g)
+            def _():
+                req_copy(zout.at[p], ag.at[h, p], s2.at[p], q2.at[p], p).wait_recv()
+
+        ship(q, 0, h, at(c, 1, 0))
+        ship(q, 1, h, at(c, 3, 0))
+        ship(q, 3, h, at(c, 0, 1))
+        ship(q, 4, h, at(c, 0, 3))
+    for c in range(2):
+        use_half(h, c)
+    for q in range(4):
+        c, odd = q // 2, q % 2
+        arrive(q, at(c, 1, 0))
+        arrive(q, at(c, 3, 0))
+        if odd:
+            ship(q, 2, at(c, 1, 0), at(c, 3, 0))
+        else:
+            ship(q, 2, at(c, 3, 0), at(c, 1, 0))
+        for j in (1, 3):
+            ship(q, 3 + 2 * j, at(c, j, 0), at(c, 0, 1))
+            ship(q, 4 + 2 * j, at(c, j, 0), at(c, 0, 3))
+    for c in range(2):
+
+        @pl.loop(0, 2)
+        def _(i):
+            use_half(at(c, 2 * i + 1, 0), c)
+
+    for q in range(4):
+        c = q // 2
+        arrive(q, at(c, 2, 0))
+        ship(q, 7, at(c, 2, 0), at(c, 0, 1))
+        ship(q, 8, at(c, 2, 0), at(c, 0, 3))
+
+    @pl.loop(0, 4)
+    def _(i):
+        j = lax.rem(i + i + i, 4)
+        for q in range(4):
+            c, odd = q // 2, q % 2
+            arrive(q, at(c, j, 1))
+            arrive(q, at(c, j, 3))
+            if odd:
+                ship(q, 11 + j, at(c, j, 1), at(c, 0, 3))
+            else:
+                ship(q, 11 + j, at(c, j, 3), at(c, 0, 1))
+
+    for c in range(2):
+        use_half(at(c, 2, 0), c)
+
+        @pl.loop(0, 4)
+        def _(j):
+            use_half(at(c, j, 1), c)
+            use_half(at(c, j, 3), c)
+
+    @pl.loop(0, 4)
+    def _(i):
+        j = lax.rem(i + i + i, 4)
+        for q in range(4):
+            arrive(q, at(q // 2, j, 2))
+        for c in range(2):
+            use_half(at(c, j, 2), c)
+
+    for side_at in range(2):
+        mean = jnp.sum(ssq[side_at], axis=1, keepdims=True) * (1.0 / width)
         inverse = lax.rsqrt(mean + 1e-05)
-        gate = jnp.minimum(acc[side, :, 0:256] * inverse + bias[:, 0:256], 7.0)
-        up = jnp.clip(acc[side, :, 256:512] * inverse + bias[:, 256:512], -7.0, 7.0)
-        act_s[side] = ((up + 1.0) * gate * jax.nn.sigmoid(1.702 * gate)).astype(BF)
-
-    def down(p):
-        return jnp.dot(
-            act_s[lax.div(p, NBLK)], wd_s[:, lanes(lax.rem(p, NBLK))], preferred_element_type=F32
+        gate = jnp.minimum(acc[side_at, :, 0:256] * inverse + bias[:, 0:256], 7.0)
+        up = jnp.clip(acc[side_at, :, 256:512] * inverse + bias[:, 256:512], -7.0, 7.0)
+        act_s[side_at] = ((up + 1.0) * gate * jax.nn.sigmoid(1.702 * gate)).astype(BF)
+
+    rowq = quart * SLOTS
+
+    def down(p, c):
+        here = slice(c * 2 * rowq, (c + 1) * 2 * rowq)
+        pout[p, here] = jnp.dot(
+            act_s[lax.div(p, NBLK), here],
+            wd_s[:, lanes(lax.rem(p, NBLK))],
+            preferred_element_type=F32,
         ).astype(BF)
 
-    @pl.loop(1, n_hid)
-    def _(d):
-        p = lax.rem(h + d, n_hid)
-        pout[p] = down(p)
-        hid_copy(pout.at[p], rs.at[h], s5.at[p], q5.at[h], p).start()
+    def part(p, q):
+        return pout.at[p, pl.ds(q * rowq, rowq)]
+
+    def load(p, q):
+        return pout[p, pl.ds(q * rowq, rowq)].astype(F32)
+
+    def pass_on(q, k, m, p, dst, peer):
+        hid_copy(part(p, q), dst, s5.at[q, k], q5.at[q, m], peer).start()
+
+    def landed(q, m, dst):
+        hid_copy(dst, dst, s5.at[q, 0], q5.at[q, m], at(0, 1, 0)).wait_recv()
+
+    @pl.loop(0, 4)
+    def _(j):
+        for c in range(2):
+            down(at(c, j, 2), c)
+        for q in range(4):
+            c, odd = q // 2, q % 2
+            peer = at(c, 0, 1) if odd else at(c, 0, 3)
+            pass_on(q, j, j, at(c, j, 2), rb1.at[q, j], peer)
+
+    @pl.loop(0, 4)
+    def _(j):
+        for c in range(2):
+            down(at(c, j, 1), c)
+            down(at(c, j, 3), c)
+        for q in range(4):
+            c, odd = q // 2, q % 2
+            to = 3 if odd else 1
+            pass_on(q, 4 + j, 4 + j, at(c, j, to), rb2.at[q, j, 0], at(c, 0, to))
+
+    @pl.loop(0, 4)
+    def _(j):
+        for q in range(4):
+            c, odd = q // 2, q % 2
+            to = 1 if odd else 3
+            p = at(c, j, to)
+            landed(q, j, rb1.at[q, j])
+            both = load(p, q) + rb1[q, j].astype(F32)
+            pout[p, pl.ds(q * rowq, rowq)] = both.astype(BF)
+            pass_on(q, 8 + j, 8 + j, p, rb2.at[q, j, 1], at(c, 0, to))
+        for c in range(2):
+            down(at(c, j, 0), c)
+
+    def line_sum(j, q):
+        landed(q, 4 + j, rb2.at[q, j, 0])
+        landed(q, 8 + j, rb2.at[q, j, 1])
+        p = at(q // 2, j, 0)
+        both = load(p, q) + rb2[q, j, 0].astype(F32) + rb2[q, j, 1].astype(F32)
+        pout[p, pl.ds(q * rowq, rowq)] = both.astype(BF)
+        return both
+
+    for q in range(4):
+        c, odd = q // 2, q % 2
+        line_sum(2, q)
+        pass_on(q, 12, 12, at(c, 2, 0), ra1.at[q], at(c, 1 if odd else 3, 0))
+    for q in range(4):
+        c, odd = q // 2, q % 2
+        to = 3 if odd else 1
+        line_sum(to, q)
+        pass_on(q, 13, 13, at(c, to, 0), ra2.at[q, 0], at(c, to, 0))
+    for q in range(4):
+        line_sum(1 if q % 2 else 3, q)
+        tot[q * rowq : (q + 1) * rowq] = line_sum(0, q)
+    for q in range(4):
+        c, odd = q // 2, q % 2
+        to = 1 if odd else 3
+        p = at(c, to, 0)
+        landed(q, 12, ra1.at[q])
+        both = load(p, q) + ra1[q].astype(F32)
+        pout[p, pl.ds(q * rowq, rowq)] = both.astype(BF)
+        pass_on(q, 14, 14, p, ra2.at[q, 1], at(c, to, 0))
 
     total_stats = stat_s[...]
     for d in range(1, NBLK):
@@ -278,23 +423,22 @@
     logits = total_stats[:, 0:experts] * row_inverse + rb_ref[...]
     raised = jnp.where(mask > 0.5, jnp.exp(jnp.where(mask > 0.5, logits, 0.0)), 0.0)
     combine = (raised / jnp.sum(raised, axis=1, keepdims=True)).astype(BF)
-    combine_wide = jnp.dot(combine, expand, preferred_element_type=F32)
+    combine_wide = dot_nt(combine, expand_t)
     weights = jnp.where(chosen > 0.5, combine_wide, 0.0).astype(BF)
 
-    def add5(d, total):
-        p = lax.rem(h - d + n_hid, n_hid)
-        hid_copy(rs.at[p], rs.at[p], s5.at[p], q5.at[p], p).wait_recv()
-        return total + rs[p].astype(F32)
-
-    summed = lax.fori_loop(1, n_hid, add5, down(h).astype(F32))
-    expert_out = summed + db_s[:, lanes(f)]
-
-    zbout[...] = expert_out.reshape(n_req, SLOTS, BLK).astype(BF)
-
-    @pl.loop(1, n_req)
-    def _(d):
-        p = lax.rem(g + d, n_req)
-        req_copy(zbout.at[p], zbin.at[g], s6.at[p], q6.at[g], p).start()
+    for q in range(4):
+        landed(q, 13, ra2.at[q, 0])
+        landed(q, 14, ra2.at[q, 1])
+        summed = tot[q * rowq : (q + 1) * rowq]
+        summed = summed + ra2[q, 0].astype(F32) + ra2[q, 1].astype(F32)
+        expert_out = summed + db_s[:, lanes(f)]
+        zbout[q * quart : (q + 1) * quart] = expert_out.reshape(quart, SLOTS, BLK).astype(BF)
+
+        @pl.loop(q * quart, (q + 1) * quart)
+        def _(p):
+            @pl.when(p != g)
+            def _():
+                req_copy(zbout.at[p], zbin.at[g], s6.at[p], q6.at[g], p).start()
 
     zbin[g] = zbout[g]
 
@@ -325,12 +469,17 @@
         both = rfin[b].astype(F32) + rfin[NBLK + b].astype(F32)
         out_ref[:, b * BLK : b * BLK + size] = both[:, :size].astype(BF)
 
+    for q in range(4):
+
+        @pl.loop(0, 15)
+        def _(k):
+            hid_copy(piece(h, q), piece(h, q), s4.at[q, k], q4.at[h, q], at(0, 1, 0)).wait_send()
+            hid_copy(part(h, q), part(h, q), s5.at[q, k], q5.at[q, k], at(0, 1, 0)).wait_send()
+
     @pl.loop(1, n_hid)
     def _(d):
         p = lax.rem(h + d, n_hid)
         hid_copy(r1.at[p], r1.at[p], s1.at[p], q1.at[p], p).wait_send()
-        hid_copy(zin, ag.at[p], s4.at[p], q4.at[p], p).wait_send()
-        hid_copy(rs.at[p], rs.at[p], s5.at[p], q5.at[p], p).wait_send()
         hid_copy(fin_s, rfin.at[p], s7.at[p], q7.at[p], p).wait_send()
 
     @pl.loop(1, NBLK)
@@ -341,7 +490,7 @@
     @pl.loop(1, n_req)
     def _(d):
         p = lax.rem(g + d, n_req)
-        req_copy(zout.at[p], zin.at[p], s2.at[p], q2.at[p], p).wait_send()
+        req_copy(zout.at[p], ag.at[h, p], s2.at[p], q2.at[p], p).wait_send()
         req_copy(zbout.at[p], zbin.at[p], s6.at[p], q6.at[p], p).wait_send()
 
 
@@ -374,23 +523,26 @@
             pltpu.VMEM((rows, wide), BF),
             pltpu.VMEM((rows, wide), BF),
             pltpu.VMEM((1, wide), F32),
-            pltpu.VMEM((wide, 128), BF),
+            pltpu.VMEM((128, wide), BF),
             pltpu.VMEM((1, wide), F32),
-            pltpu.VMEM(gate_up.shape[1:], BF),
+            pltpu.VMEM(gate_up.shape[:0:-1], BF),
             pltpu.VMEM(down_weight.shape[1:], BF),
-            pltpu.VMEM((wide, 512), BF),
+            pltpu.VMEM((512, wide), BF),
             pltpu.VMEM((256, wide), BF),
             pltpu.VMEM((n_hid, rows, BLK), BF),
             pltpu.VMEM((rows, 128), F32),
             pltpu.VMEM((NBLK, rows, 128), F32),
-            pltpu.VMEM((n_req, SLOTS, BLK), BF),
             pltpu.VMEM((n_req, SLOTS, BLK), BF),
             pltpu.VMEM((n_hid, n_req, SLOTS, BLK), BF),
             pltpu.VMEM((2, per, 512), F32),
             pltpu.VMEM((2, per, 128), F32),
             pltpu.VMEM((2, per, 256), BF),
             pltpu.VMEM((n_hid, per, BLK), BF),
-            pltpu.VMEM((n_hid, per, BLK), BF),
+            pltpu.VMEM((per, BLK), F32),
+            pltpu.VMEM((4, 4, per // 4, BLK), BF),
+            pltpu.VMEM((4, 4, 2, per // 4, BLK), BF),
+            pltpu.VMEM((4, per // 4, BLK), BF),
+            pltpu.VMEM((4, 2, per // 4, BLK), BF),
             pltpu.VMEM((n_req, SLOTS, BLK), BF),
             pltpu.VMEM((n_req, SLOTS, BLK), BF),
             pltpu.VMEM((rows, BLK), BF),
@@ -402,10 +554,10 @@
             req_sem,
             dma((NBLK,)),
             dma((NBLK,)),
-            hid_sem,
-            hid_sem,
-            hid_sem,
-            hid_sem,
+            dma((4, 15)),
+            dma((n_hid, 4)),
+            dma((4, 15)),
+            dma((4, 15)),
             req_sem,
             req_sem,
             hid_sem,
@@ -419,12 +571,12 @@
         attn_partial[0],
         residual,
         norm_gain.reshape(1, width),
-        router_weight,
+        router_weight.T,
         router_bias.reshape(1, -1),
-        routes,
+        routes.T,
         gate_up_bias,
         down_bias,
-        gate_up[0],
+        gate_up[0].T,
         down_weight[0],
     )
 

time: 203 us -> 118 us (0.58); the launches traced: 200 us -> 117 us
  Pallas kernels: 189 us -> 114 us
  local copies, waits for them, and re-layouts: 10.6 us -> 3.05 us
    pallas_call x1, Pallas kernels: 189 us -> 114 us  [on_device(): pl.pallas_call(functools.partial(moe_kernel, n_req, n_hid), out_shape=jax...]
    unnamed x4 -> x1, local copies, waits for them, and re-layouts: 9.33 us -> 1.76 us
where the time goes in v2:
time: 118 us; the launch traced here: 117 us
  Pallas kernels  114 us (97%)
  local copies, waits for them, and re-layouts  3.05 us (3%)
    pallas_call x1, Pallas kernels, on_device(): pl.pallas_call(functools.partial(moe_kernel, n_req, n_hid), out_shape=jax...  114 us

profile of v2, /device:TPU:1, one launch (start us, length us, event | category | flops | bytes accessed | tf_op | source)
XLA Modules:
  0.0 117.4 jit_solution(3168919097126665850)
XLA Ops:
  0.0 1.3 %reshape.6.gain_ref = bf16[1,2880]{1,0:T(2,128)(2,1)} reshape(bf16[2880]{0:T(1024)(128)(2,1)} %param.12) | data formatting | bytes 11520 | tf_op jit(solution)/shard_map/reshape | solution.py:573
  1.3 114.3 %moe_block.1 = bf16[64,2880]{1,0:T(8,128)(2,1)} custom-call(bf16[64,2880]{1,0:T(8,128)(2,1)} %bitcast.10, bf16[64,2880]{1,0:T(8,128)(2,1)} %resid_ref.1, bf16[1,2880]{1,0:T(2,128)(2,1)} %reshape.6.gain_ref, bf16[32,2880]{1,0:T(8,128)(2,1)} %bitcast.11, f32[1,32]{1,0:T(1,128)} %bitcast.13, s32[4,64]{1,0:T(4,128)} %bitcast.12, bf16[1,360]{1,0:T(2,128)(2,1)} %bgu_ref.1, ...), custom_call_target="tpu_custom_call" | custom-call | tf_op jit(solution)/shard_map/moe_block/pallas_call | solution.py:517
  115.6 1.8 %copy.12 = bf16[64,2880]{1,0:T(8,128)(2,1)} copy(bf16[64,2880]{1,0:T(8,128)(2,1)} %moe_block.1) | data formatting | bytes 737280

commit v3 on v2

--- a/solution.py
+++ b/solution.py
@@ -48,7 +48,12 @@
     wd_v,
     wg_s,
     wd_s,
-    r1,
+    mid1,
+    sum1,
+    rb1_1,
+    rb2_1,
+    ra1_1,
+    ra2_1,
     stat_s,
     rstat,
     zout,
@@ -57,14 +62,14 @@
     ssq,
     act_s,
     pout,
-    tot,
+    mid5,
+    sum5,
     rb1,
     rb2,
     ra1,
     ra2,
     zbout,
     zbin,
-    fin_s,
     rfin,
     w_sem,
     s1,
@@ -116,7 +121,7 @@
     resid_s[:, tail:] = jnp.zeros((rows, wide - tail), BF)
     resid_s[:, :width] = resid_ref[...]
     gain_s[:, tail:] = jnp.zeros((1, wide - tail), F32)
-    gain_s[:, :width] = gain_ref[...].astype(F32)
+    gain_s[:, :width] = gain_ref[...].reshape(1, width).astype(F32)
     db_s[:, tail:] = jnp.zeros((1, wide - tail), F32)
     db_s[:, :width] = db_ref[...].astype(F32)
 
@@ -142,11 +147,180 @@
             device_id_type=MESH,
         )
 
-    @pl.loop(1, n_hid)
-    def _(d):
-        p = lax.rem(h + d, n_hid)
-        src = attn_s.at[:, lanes(lax.rem(p, NBLK))]
-        hid_copy(src, r1.at[h], s1.at[p], q1.at[h], p).start()
+    side = 4
+    x = lax.div(h, side)
+    y = lax.rem(h, side)
+
+    def at(c, da, db):
+        a = lax.rem((x if c == 0 else y) + da, side)
+        b = lax.rem((y if c == 0 else x) + db, side)
+        return a * side + b if c == 0 else b * side + a
+
+    def scatter_first(src, bufs, sems, make):
+        rb1 = bufs[2]
+        rb2 = bufs[3]
+
+        def send(q, k, ref, dst, peer):
+            hid_copy(ref, dst, sems[0].at[q, k], sems[1].at[q, k], peer).start()
+
+        @pl.loop(0, 4)
+        def _(j):
+            for c in range(2):
+                make(at(c, j, 2), c)
+            for q in range(4):
+                c, odd = q // 2, q % 2
+                peer = at(c, 0, 1) if odd else at(c, 0, 3)
+                send(q, j, src(at(c, j, 2), q), rb1.at[q, j], peer)
+
+        @pl.loop(0, 4)
+        def _(j):
+            for c in range(2):
+                make(at(c, j, 1), c)
+                make(at(c, j, 3), c)
+            for q in range(4):
+                c, odd = q // 2, q % 2
+                to = 3 if odd else 1
+                send(q, 4 + j, src(at(c, j, to), q), rb2.at[q, j, 0], at(c, 0, to))
+
+    def scatter_rest(src, bufs, sems, make):
+        mid, sums, rb1, rb2, ra1, ra2 = bufs
+
+        def send(q, k, ref, dst, peer):
+            hid_copy(ref, dst, sems[0].at[q, k], sems[1].at[q, k], peer).start()
+
+        def landed(q, k, dst):
+            hid_copy(dst, dst, sems[0].at[q, 0], sems[1].at[q, k], at(0, 1, 0)).wait_recv()
+
+        @pl.loop(0, 4)
+        def _(j):
+            for q in range(4):
+                c, odd = q // 2, q % 2
+                to = 1 if odd else 3
+                landed(q, j, rb1.at[q, j])
+                both = src(at(c, j, to), q)[...].astype(F32) + rb1[q, j].astype(F32)
+                mid[q, j] = both.astype(BF)
+                send(q, 8 + j, mid.at[q, j], rb2.at[q, j, 1], at(c, 0, to))
+            for c in range(2):
+                make(at(c, j, 0), c)
+
+        def line_sum(j, q):
+            landed(q, 4 + j, rb2.at[q, j, 0])
+            landed(q, 8 + j, rb2.at[q, j, 1])
+            three = src(at(q // 2, j, 0), q)[...].astype(F32)
+            return three + rb2[q, j, 0].astype(F32) + rb2[q, j, 1].astype(F32)
+
+        for q in range(4):
+            c, odd = q // 2, q % 2
+            sums[q, 2] = line_sum(2, q).astype(BF)
+            send(q, 12, sums.at[q, 2], ra1.at[q], at(c, 1 if odd else 3, 0))
+        for q in range(4):
+            c, odd = q // 2, q % 2
+            to = 3 if odd else 1
+            sums[q, to] = line_sum(to, q).astype(BF)
+            send(q, 13, sums.at[q, to], ra2.at[q, 0], at(c, to, 0))
+        for q in range(4):
+            c, odd = q // 2, q % 2
+            to = 1 if odd else 3
+            near = line_sum(to, q)
+            landed(q, 12, ra1.at[q])
+            sums[q, to] = (near + ra1[q].astype(F32)).astype(BF)
+            send(q, 14, sums.at[q, to], ra2.at[q, 1], at(c, to, 0))
+
+        def result(q):
+            total = line_sum(0, q)
+            landed(q, 13, ra2.at[q, 0])
+            landed(q, 14, ra2.at[q, 1])
+            return total + ra2[q, 0].astype(F32) + ra2[q, 1].astype(F32)
+
+        return result
+
+    def gather_over_hid(piece, sems, ready, after):
+        def ship(q, k, p, peer):
+            ref = piece(p, q)
+            hid_copy(ref, ref, sems[0].at[q, k], sems[1].at[p, q], peer).start()
+
+        def arrive(q, p):
+            ref = piece(p, q)
+            hid_copy(ref, ref, sems[0].at[q, 0], sems[1].at[p, q], p).wait_recv()
+
+        for q in range(4):
+            c = q // 2
+            ready(q)
+            ship(q, 0, h, at(c, 1, 0))
+            ship(q, 1, h, at(c, 3, 0))
+            ship(q, 3, h, at(c, 0, 1))
+            ship(q, 4, h, at(c, 0, 3))
+        for c in range(2):
+            after(h, c)
+        for q in range(4):
+            c, odd = q // 2, q % 2
+            arrive(q, at(c, 1, 0))
+            arrive(q, at(c, 3, 0))
+            if odd:
+                ship(q, 2, at(c, 1, 0), at(c, 3, 0))
+            else:
+                ship(q, 2, at(c, 3, 0), at(c, 1, 0))
+            for j in (1, 3):
+                ship(q, 3 + 2 * j, at(c, j, 0), at(c, 0, 1))
+                ship(q, 4 + 2 * j, at(c, j, 0), at(c, 0, 3))
+        for c in range(2):
+
+            @pl.loop(0, 2)
+            def _(i):
+                after(at(c, 2 * i + 1, 0), c)
+
+        for q in range(4):
+            c = q // 2
+            arrive(q, at(c, 2, 0))
+            ship(q, 7, at(c, 2, 0), at(c, 0, 1))
+            ship(q, 8, at(c, 2, 0), at(c, 0, 3))
+
+        @pl.loop(0, 4)
+        def _(i):
+            j = lax.rem(i + i + i, 4)
+            for q in range(4):
+                c, odd = q // 2, q % 2
+                arrive(q, at(c, j, 1))
+                arrive(q, at(c, j, 3))
+                if odd:
+                    ship(q, 11 + j, at(c, j, 1), at(c, 0, 3))
+                else:
+                    ship(q, 11 + j, at(c, j, 3), at(c, 0, 1))
+
+        for c in range(2):
+            after(at(c, 2, 0), c)
+
+            @pl.loop(0, 4)
+            def _(j):
+                after(at(c, j, 1), c)
+                after(at(c, j, 3), c)
+
+        @pl.loop(0, 4)
+        def _(i):
+            j = lax.rem(i + i + i, 4)
+            for q in range(4):
+                arrive(q, at(q // 2, j, 2))
+            for c in range(2):
+                after(at(c, j, 2), c)
+
+    def sent(refs, sems):
+        for q in range(4):
+
+            @pl.loop(0, 15)
+            def _(k):
+                ref = refs(q)
+                hid_copy(ref, ref, sems[0].at[q, k], sems[0].at[q, k], at(0, 1, 0)).wait_send()
+
+    def nothing(p, c):
+        pass
+
+    bufs1 = (mid1, sum1, rb1_1, rb2_1, ra1_1, ra2_1)
+    rowq1 = rows // 4
+
+    def share(p, q):
+        return attn_s.at[pl.ds(q * rowq1, rowq1), lanes(lax.rem(p, NBLK))]
+
+    scatter_first(share, bufs1, (s1, q1), nothing)
 
     wr_s[...] = jnp.zeros(wr_s.shape, BF)
     wr_s[0:experts, 0:width] = wr_ref[...]
@@ -171,12 +345,8 @@
     chosen = dot_nt(same, chosen_t)
     mask = dot_nt(same, mask_t)
 
-    def add1(d, total):
-        p = lax.rem(h - d + n_hid, n_hid)
-        hid_copy(r1.at[p], r1.at[p], s1.at[p], q1.at[p], p).wait_recv()
-        return total + r1[p].astype(F32)
-
-    attention = lax.fori_loop(1, n_hid, add1, attn_s[:, lanes(f)].astype(F32))
+    result1 = scatter_rest(share, bufs1, (s1, q1), nothing)
+    attention = jnp.concatenate([result1(q) for q in range(4)], axis=0)
     stream = (resid_s[:, lanes(f)].astype(F32) + attention).astype(BF)
     stream_wide = stream.astype(F32)
 
@@ -184,7 +354,9 @@
     zout[...] = picked.reshape(experts, SLOTS, BLK).astype(BF)
 
     @pl.loop(1, n_req)
-    def _(d):
+    def _(i):
+        step = lax.div(i + 1, 2)
+        d = step + lax.rem(i + 1, 2) * (n_req - 2 * step)
         p = lax.rem(g + d, n_req)
         req_copy(zout.at[p], ag.at[h, g], s2.at[p], q2.at[g], p).start()
 
@@ -224,104 +396,39 @@
     acc[...] = jnp.zeros(acc.shape, F32)
     ssq[...] = jnp.zeros(ssq.shape, F32)
 
-    side = 4
-    x = lax.div(h, side)
-    y = lax.rem(h, side)
-
-    def at(c, da, db):
-        a = lax.rem((x if c == 0 else y) + da, side)
-        b = lax.rem((y if c == 0 else x) + db, side)
-        return a * side + b if c == 0 else b * side + a
-
     quart = n_req // 4
+    half0 = lax.div(g, 2 * quart)
+
+    def group_at(q):
+        return lax.rem(half0 + q // 2, 2) * (2 * quart) + q % 2 * quart
 
     def piece(p, q):
-        return ag.at[p, pl.ds(q * quart, quart)]
-
-    def ship(q, k, p, peer):
-        hid_copy(piece(p, q), piece(p, q), s4.at[q, k], q4.at[p, q], peer).start()
-
-    def arrive(q, p):
-        hid_copy(piece(p, q), piece(p, q), s4.at[q, 0], q4.at[p, q], p).wait_recv()
+        return ag.at[p, pl.ds(group_at(q), quart)]
 
     def use_half(p, c):
-        wide_rows = ag[p, c * 2 * quart : (c + 1) * 2 * quart].astype(F32)
+        first = group_at(2 * c)
+        wide_rows = ag[p, pl.ds(first, 2 * quart)].astype(F32)
         count = 2 * quart * SLOTS
         wide_rows = wide_rows.reshape(count, BLK)
         to = lax.div(p, NBLK)
         blk = lax.rem(p, NBLK)
         sq = wide_rows * wide_rows
-        here = slice(c * count, (c + 1) * count)
+        here = pl.ds(pl.multiple_of(first * SLOTS, count), count)
         ssq[to, here] += sq[:, 0:128] + sq[:, 128:256] + sq[:, 256:384]
         u = (wide_rows * gain_s[:, lanes(blk)]).astype(BF)
         acc[to, here] += dot_nt(u, wg_s[:, lanes(blk)])
 
-    ag[h, g] = zout[g]
-    for q in range(4):
-        c = q // 2
-
-        @pl.loop(q * quart, (q + 1) * quart)
-        def _(p):
+    def arrived(q):
+        @pl.loop(0, quart)
+        def _(i):
+            p = group_at(q) + i
+
             @pl.when(p != g)
             def _():
                 req_copy(zout.at[p], ag.at[h, p], s2.at[p], q2.at[p], p).wait_recv()
 
-        ship(q, 0, h, at(c, 1, 0))
-        ship(q, 1, h, at(c, 3, 0))
-        ship(q, 3, h, at(c, 0, 1))
-        ship(q, 4, h, at(c, 0, 3))
-    for c in range(2):
-        use_half(h, c)
-    for q in range(4):
-        c, odd = q // 2, q % 2
-        arrive(q, at(c, 1, 0))
-        arrive(q, at(c, 3, 0))
-        if odd:
-            ship(q, 2, at(c, 1, 0), at(c, 3, 0))
-        else:
-            ship(q, 2, at(c, 3, 0), at(c, 1, 0))
-        for j in (1, 3):
-            ship(q, 3 + 2 * j, at(c, j, 0), at(c, 0, 1))
-            ship(q, 4 + 2 * j, at(c, j, 0), at(c, 0, 3))
-    for c in range(2):
-
-        @pl.loop(0, 2)
-        def _(i):
-            use_half(at(c, 2 * i + 1, 0), c)
-
-    for q in range(4):
-        c = q // 2
-        arrive(q, at(c, 2, 0))
-        ship(q, 7, at(c, 2, 0), at(c, 0, 1))
-        ship(q, 8, at(c, 2, 0), at(c, 0, 3))
-
-    @pl.loop(0, 4)
-    def _(i):
-        j = lax.rem(i + i + i, 4)
-        for q in range(4):
-            c, odd = q // 2, q % 2
-            arrive(q, at(c, j, 1))
-            arrive(q, at(c, j, 3))
-            if odd:
-                ship(q, 11 + j, at(c, j, 1), at(c, 0, 3))
-            else:
-                ship(q, 11 + j, at(c, j, 3), at(c, 0, 1))
-
-    for c in range(2):
-        use_half(at(c, 2, 0), c)
-
-        @pl.loop(0, 4)
-        def _(j):
-            use_half(at(c, j, 1), c)
-            use_half(at(c, j, 3), c)
-
-    @pl.loop(0, 4)
-    def _(i):
-        j = lax.rem(i + i + i, 4)
-        for q in range(4):
-            arrive(q, at(q // 2, j, 2))
-        for c in range(2):
-            use_half(at(c, j, 2), c)
+    ag[h, g] = zout[g]
+    gather_over_hid(piece, (s4, q4), arrived, use_half)
 
     for side_at in range(2):
         mean = jnp.sum(ssq[side_at], axis=1, keepdims=True) * (1.0 / width)
@@ -343,75 +450,9 @@
     def part(p, q):
         return pout.at[p, pl.ds(q * rowq, rowq)]
 
-    def load(p, q):
-        return pout[p, pl.ds(q * rowq, rowq)].astype(F32)
-
-    def pass_on(q, k, m, p, dst, peer):
-        hid_copy(part(p, q), dst, s5.at[q, k], q5.at[q, m], peer).start()
-
-    def landed(q, m, dst):
-        hid_copy(dst, dst, s5.at[q, 0], q5.at[q, m], at(0, 1, 0)).wait_recv()
-
-    @pl.loop(0, 4)
-    def _(j):
-        for c in range(2):
-            down(at(c, j, 2), c)
-        for q in range(4):
-            c, odd = q // 2, q % 2
-            peer = at(c, 0, 1) if odd else at(c, 0, 3)
-            pass_on(q, j, j, at(c, j, 2), rb1.at[q, j], peer)
-
-    @pl.loop(0, 4)
-    def _(j):
-        for c in range(2):
-            down(at(c, j, 1), c)
-            down(at(c, j, 3), c)
-        for q in range(4):
-            c, odd = q // 2, q % 2
-            to = 3 if odd else 1
-            pass_on(q, 4 + j, 4 + j, at(c, j, to), rb2.at[q, j, 0], at(c, 0, to))
-
-    @pl.loop(0, 4)
-    def _(j):
-        for q in range(4):
-            c, odd = q // 2, q % 2
-            to = 1 if odd else 3
-            p = at(c, j, to)
-            landed(q, j, rb1.at[q, j])
-            both = load(p, q) + rb1[q, j].astype(F32)
-            pout[p, pl.ds(q * rowq, rowq)] = both.astype(BF)
-            pass_on(q, 8 + j, 8 + j, p, rb2.at[q, j, 1], at(c, 0, to))
-        for c in range(2):
-            down(at(c, j, 0), c)
-
-    def line_sum(j, q):
-        landed(q, 4 + j, rb2.at[q, j, 0])
-        landed(q, 8 + j, rb2.at[q, j, 1])
-        p = at(q // 2, j, 0)
-        both = load(p, q) + rb2[q, j, 0].astype(F32) + rb2[q, j, 1].astype(F32)
-        pout[p, pl.ds(q * rowq, rowq)] = both.astype(BF)
-        return both
-
-    for q in range(4):
-        c, odd = q // 2, q % 2
-        line_sum(2, q)
-        pass_on(q, 12, 12, at(c, 2, 0), ra1.at[q], at(c, 1 if odd else 3, 0))
-    for q in range(4):
-        c, odd = q // 2, q % 2
-        to = 3 if odd else 1
-        line_sum(to, q)
-        pass_on(q, 13, 13, at(c, to, 0), ra2.at[q, 0], at(c, to, 0))
-    for q in range(4):
-        line_sum(1 if q % 2 else 3, q)
-        tot[q * rowq : (q + 1) * rowq] = line_sum(0, q)
-    for q in range(4):
-        c, odd = q // 2, q % 2
-        to = 1 if odd else 3
-        p = at(c, to, 0)
-        landed(q, 12, ra1.at[q])
-        both = load(p, q) + ra1[q].astype(F32)
-        pout[p, pl.ds(q * rowq, rowq)] = both.astype(BF)
-        pass_on(q, 14, 14, p, ra2.at[q, 1], at(c, to, 0))
+    bufs5 = (mid5, sum5, rb1, rb2, ra1, ra2)
+    scatter_first(part, bufs5, (s5, q5), down)
+    result5 = scatter_rest(part, bufs5, (s5, q5), down)
 
     total_stats = stat_s[...]
     for d in range(1, NBLK):
@@ -427,11 +468,7 @@
     weights = jnp.where(chosen > 0.5, combine_wide, 0.0).astype(BF)
 
     for q in range(4):
-        landed(q, 13, ra2.at[q, 0])
-        landed(q, 14, ra2.at[q, 1])
-        summed = tot[q * rowq : (q + 1) * rowq]
-        summed = summed + ra2[q, 0].astype(F32) + ra2[q, 1].astype(F32)
-        expert_out = summed + db_s[:, lanes(f)]
+        expert_out = result5(q) + db_s[:, lanes(f)]
         zbout[q * quart : (q + 1) * quart] = expert_out.reshape(quart, SLOTS, BLK).astype(BF)
 
         @pl.loop(q * quart, (q + 1) * quart)
@@ -450,37 +487,22 @@
     returned = zbin[...].astype(F32).reshape(pairs, BLK).astype(BF)
     mixture = jnp.dot(weights, returned, preferred_element_type=F32)
     first = jnp.where(sg == 0, 1.0, 0.0)
-    fin_s[...] = (mixture + stream_wide * first).astype(BF)
-
-    @pl.loop(1, n_hid)
-    def _(d):
-        p = lax.rem(h + d, n_hid)
-        hid_copy(fin_s, rfin.at[h], s7.at[p], q7.at[h], p).start()
-
-    rfin[h] = fin_s[...]
-
-    @pl.loop(1, n_hid)
-    def _(d):
-        p = lax.rem(h - d + n_hid, n_hid)
-        hid_copy(rfin.at[p], rfin.at[p], s7.at[p], q7.at[p], p).wait_recv()
+    rfin[h] = (mixture + stream_wide * first).astype(BF)
+
+    def final(p, q):
+        return rfin.at[p, pl.ds(q * rowq1, rowq1)]
+
+    gather_over_hid(final, (s7, q7), lambda q: None, nothing)
 
     for b in range(NBLK):
         size = min(BLK, width - b * BLK)
         both = rfin[b].astype(F32) + rfin[NBLK + b].astype(F32)
         out_ref[:, b * BLK : b * BLK + size] = both[:, :size].astype(BF)
 
-    for q in range(4):
-
-        @pl.loop(0, 15)
-        def _(k):
-            hid_copy(piece(h, q), piece(h, q), s4.at[q, k], q4.at[h, q], at(0, 1, 0)).wait_send()
-            hid_copy(part(h, q), part(h, q), s5.at[q, k], q5.at[q, k], at(0, 1, 0)).wait_send()
-
-    @pl.loop(1, n_hid)
-    def _(d):
-        p = lax.rem(h + d, n_hid)
-        hid_copy(r1.at[p], r1.at[p], s1.at[p], q1.at[p], p).wait_send()
-        hid_copy(fin_s, rfin.at[p], s7.at[p], q7.at[p], p).wait_send()
+    sent(lambda q: share(h, q), (s1, q1))
+    sent(lambda q: piece(h, q), (s4, q4))
+    sent(lambda q: part(h, q), (s5, q5))
+    sent(lambda q: final(h, q), (s7, q7))
 
     @pl.loop(1, NBLK)
     def _(d):
@@ -492,6 +514,17 @@
         p = lax.rem(g + d, n_req)
         req_copy(zout.at[p], ag.at[h, p], s2.at[p], q2.at[p], p).wait_send()
         req_copy(zbout.at[p], zbin.at[p], s6.at[p], q6.at[p], p).wait_send()
+
+
+def ring_buffers(size):
+    return [
+        pltpu.VMEM((4, 4, size, BLK), BF),
+        pltpu.VMEM((4, 4, size, BLK), BF),
+        pltpu.VMEM((4, 4, size, BLK), BF),
+        pltpu.VMEM((4, 4, 2, size, BLK), BF),
+        pltpu.VMEM((4, size, BLK), BF),
+        pltpu.VMEM((4, 2, size, BLK), BF),
+    ]
 
 
 def on_device(
@@ -529,7 +562,7 @@
             pltpu.VMEM(down_weight.shape[1:], BF),
             pltpu.VMEM((512, wide), BF),
             pltpu.VMEM((256, wide), BF),
-            pltpu.VMEM((n_hid, rows, BLK), BF),
+            *ring_buffers(rows // 4),
             pltpu.VMEM((rows, 128), F32),
             pltpu.VMEM((NBLK, rows, 128), F32),
             pltpu.VMEM((n_req, SLOTS, BLK), BF),
@@ -538,18 +571,13 @@
             pltpu.VMEM((2, per, 128), F32),
             pltpu.VMEM((2, per, 256), BF),
             pltpu.VMEM((n_hid, per, BLK), BF),
-            pltpu.VMEM((per, BLK), F32),
-            pltpu.VMEM((4, 4, per // 4, BLK), BF),
-            pltpu.VMEM((4, 4, 2, per // 4, BLK), BF),
-            pltpu.VMEM((4, per // 4, BLK), BF),
-            pltpu.VMEM((4, 2, per // 4, BLK), BF),
+            *ring_buffers(per // 4),
             pltpu.VMEM((n_req, SLOTS, BLK), BF),
             pltpu.VMEM((n_req, SLOTS, BLK), BF),
-            pltpu.VMEM((rows, BLK), BF),
             pltpu.VMEM((n_hid, rows, BLK), BF),
             dma((2,)),
-            hid_sem,
-            hid_sem,
+            dma((4, 15)),
+            dma((4, 15)),
             req_sem,
             req_sem,
             dma((NBLK,)),
@@ -560,8 +588,8 @@
             dma((4, 15)),
             req_sem,
             req_sem,
-            hid_sem,
-            hid_sem,
+            dma((4, 15)),
+            dma((n_hid, 4)),
         ],
         compiler_params=pltpu.CompilerParams(
             collective_id=0, has_side_effects=True, vmem_limit_bytes=56 * 1024 * 1024
@@ -570,7 +598,7 @@
     )(
         attn_partial[0],
         residual,
-        norm_gain.reshape(1, width),
+        norm_gain,
         router_weight.T,
         router_bias.reshape(1, -1),
         routes.T,

time: 118 us -> 116 us (0.983)
  local copies, waits for them, and re-layouts: 3.05 us -> 1.76 us
    pallas_call x1, Pallas kernels: 114 us -> 113 us  [on_device(): pl.pallas_call(functools.partial(moe_kernel, n_req, n_hid), out_shape=jax...]
    reshape x1 -> x0, local copies, waits for them, and re-layouts: 1.3 us -> none  [on_device(): norm_gain.reshape(1, width)]
where the time goes in v3:
time: 116 us; the launch traced here: 114 us
  Pallas kernels  113 us (97%)
  local copies, waits for them, and re-layouts  1.76 us (2%)
    pallas_call x1, Pallas kernels, on_device(): pl.pallas_call(functools.partial(moe_kernel, n_req, n_hid), out_shape=jax...  113 us

profile of v3, /device:TPU:1, one launch (start us, length us, event | category | flops | bytes accessed | tf_op | source)
XLA Modules:
  0.0 114.3 jit_solution(6672923818121825632)
XLA Ops:
  0.0 112.5 %moe_block.1 = bf16[64,2880]{1,0:T(8,128)(2,1)} custom-call(bf16[64,2880]{1,0:T(8,128)(2,1)} %bitcast.10, bf16[64,2880]{1,0:T(8,128)(2,1)} %resid_ref.1, bf16[2880]{0:T(1024)(128)(2,1)} %gain_ref.1, bf16[32,2880]{1,0:T(8,128)(2,1)} %bitcast.11, f32[1,32]{1,0:T(1,128)} %bitcast.13, s32[4,64]{1,0:T(4,128)} %bitcast.12, bf16[1,360]{1,0:T(2,128)(2,1)} %bgu_ref.1, ...), custom_call_target="tpu_custom_call" | custom-call | tf_op jit(solution)/shard_map/moe_block/pallas_call | solution.py:550
  112.5 1.8 %copy.12 = bf16[64,2880]{1,0:T(8,128)(2,1)} copy(bf16[64,2880]{1,0:T(8,128)(2,1)} %moe_block.1) | data formatting | bytes 737280

commit v4 on v3

--- a/solution.py
+++ b/solution.py
@@ -28,8 +28,8 @@
 def moe_kernel(
     n_req,
     n_hid,
-    attn_ref,
-    resid_ref,
+    attn_hbm,
+    resid_hbm,
     gain_ref,
     wr_ref,
     rb_ref,
@@ -39,6 +39,8 @@
     wgu_hbm,
     wd_hbm,
     out_ref,
+    attn_v,
+    resid_v,
     attn_s,
     resid_s,
     gain_s,
@@ -87,7 +89,7 @@
     s7,
     q7,
 ):
-    rows, width = attn_ref.shape
+    rows, width = attn_hbm.shape
     experts = rb_ref.shape[1]
     half = wd_hbm.shape[0]
     wide = BLK * NBLK
@@ -97,12 +99,24 @@
     sg = lax.div(h, NBLK)
     f = lax.rem(h, NBLK)
 
+    get_attn = pltpu.make_async_copy(attn_hbm, attn_v, w_sem.at[2])
+    get_resid = pltpu.make_async_copy(resid_hbm, resid_v, w_sem.at[3])
+    get_attn.start()
+    get_resid.start()
     get_wgu = pltpu.make_async_copy(wgu_hbm, wgu_v, w_sem.at[0])
     get_wd = pltpu.make_async_copy(wd_hbm, wd_v, w_sem.at[1])
     get_wgu.start()
     get_wd.start()
 
     barrier = pltpu.get_barrier_semaphore()
+
+    @pl.loop(1, n_req)
+    def _(i):
+        step = lax.div(n_req + 1 - i, 2)
+        d = step + lax.rem(n_req + 1 - i, 2) * (n_req - 2 * step)
+        pl.semaphore_signal(
+            barrier, inc=1, device_id={"req": lax.rem(g + d, n_req)}, device_id_type=MESH
+        )
 
     @pl.loop(1, n_hid)
     def _(d):
@@ -110,16 +124,12 @@
             barrier, inc=1, device_id={"hid": lax.rem(h + d, n_hid)}, device_id_type=MESH
         )
 
-    @pl.loop(1, n_req)
-    def _(d):
-        pl.semaphore_signal(
-            barrier, inc=1, device_id={"req": lax.rem(g + d, n_req)}, device_id_type=MESH
-        )
-
     attn_s[:, tail:] = jnp.zeros((rows, wide - tail), BF)
-    attn_s[:, :width] = attn_ref[...]
+    get_attn.wait()
+    attn_s[:, :width] = attn_v[...]
     resid_s[:, tail:] = jnp.zeros((rows, wide - tail), BF)
-    resid_s[:, :width] = resid_ref[...]
+    get_resid.wait()
+    resid_s[:, :width] = resid_v[...]
     gain_s[:, tail:] = jnp.zeros((1, wide - tail), F32)
     gain_s[:, :width] = gain_ref[...].reshape(1, width).astype(F32)
     db_s[:, tail:] = jnp.zeros((1, wide - tail), F32)
@@ -427,6 +437,7 @@
             def _():
                 req_copy(zout.at[p], ag.at[h, p], s2.at[p], q2.at[p], p).wait_recv()
 
+    sent(lambda q: share(h, q), (s1, q1))
     ag[h, g] = zout[g]
     gather_over_hid(piece, (s4, q4), arrived, use_half)
 
@@ -452,8 +463,6 @@
 
     bufs5 = (mid5, sum5, rb1, rb2, ra1, ra2)
     scatter_first(part, bufs5, (s5, q5), down)
-    result5 = scatter_rest(part, bufs5, (s5, q5), down)
-
     total_stats = stat_s[...]
     for d in range(1, NBLK):
         pf = lax.rem(f - d + NBLK, NBLK)
@@ -467,6 +476,8 @@
     combine_wide = dot_nt(combine, expand_t)
     weights = jnp.where(chosen > 0.5, combine_wide, 0.0).astype(BF)
 
+    result5 = scatter_rest(part, bufs5, (s5, q5), down)
+
     for q in range(4):
         expert_out = result5(q) + db_s[:, lanes(f)]
         zbout[q * quart : (q + 1) * quart] = expert_out.reshape(quart, SLOTS, BLK).astype(BF)
@@ -479,6 +490,19 @@
 
     zbin[g] = zbout[g]
 
+    sent(lambda q: piece(h, q), (s4, q4))
+    sent(lambda q: part(h, q), (s5, q5))
+
+    @pl.loop(1, NBLK)
+    def _(d):
+        pf = lax.rem(f + d, NBLK)
+        hid_copy(stat_s, rstat.at[pf], s3.at[pf], q3.at[pf], sg * NBLK + pf).wait_send()
+
+    @pl.loop(1, n_req)
+    def _(d):
+        p = lax.rem(g + d, n_req)
+        req_copy(zout.at[p], ag.at[h, p], s2.at[p], q2.at[p], p).wait_send()
+
     @pl.loop(1, n_req)
     def _(d):
         p = lax.rem(g - d + n_req, n_req)
@@ -492,28 +516,26 @@
     def final(p, q):
         return rfin.at[p, pl.ds(q * rowq1, rowq1)]
 
-    gather_over_hid(final, (s7, q7), lambda q: None, nothing)
+    finished = []
+
+    def wait_back(p, c):
+        if finished:
+            return
+        finished.append(True)
+
+        @pl.loop(1, n_req)
+        def _(d):
+            p = lax.rem(g + d, n_req)
+            req_copy(zbout.at[p], zbin.at[p], s6.at[p], q6.at[p], p).wait_send()
+
+    gather_over_hid(final, (s7, q7), lambda q: None, wait_back)
 
     for b in range(NBLK):
         size = min(BLK, width - b * BLK)
         both = rfin[b].astype(F32) + rfin[NBLK + b].astype(F32)
         out_ref[:, b * BLK : b * BLK + size] = both[:, :size].astype(BF)
 
-    sent(lambda q: share(h, q), (s1, q1))
-    sent(lambda q: piece(h, q), (s4, q4))
-    sent(lambda q: part(h, q), (s5, q5))
     sent(lambda q: final(h, q), (s7, q7))
-
-    @pl.loop(1, NBLK)
-    def _(d):
-        pf = lax.rem(f + d, NBLK)
-        hid_copy(stat_s, rstat.at[pf], s3.at[pf], q3.at[pf], sg * NBLK + pf).wait_send()
-
-    @pl.loop(1, n_req)
-    def _(d):
-        p = lax.rem(g + d, n_req)
-        req_copy(zout.at[p], ag.at[h, p], s2.at[p], q2.at[p], p).wait_send()
-        req_copy(zbout.at[p], zbin.at[p], s6.at[p], q6.at[p], p).wait_send()
 
 
 def ring_buffers(size):
@@ -550,9 +572,11 @@
     return pl.pallas_call(
         functools.partial(moe_kernel, n_req, n_hid),
         out_shape=jax.ShapeDtypeStruct((rows, width), BF),
-        in_specs=[vmem] * 8 + [hbm] * 2,
+        in_specs=[hbm] * 2 + [vmem] * 6 + [hbm] * 2,
         out_specs=vmem,
         scratch_shapes=[
+            pltpu.VMEM((rows, width), BF),
+            pltpu.VMEM((rows, width), BF),
             pltpu.VMEM((rows, wide), BF),
             pltpu.VMEM((rows, wide), BF),
             pltpu.VMEM((1, wide), F32),
@@ -575,7 +599,7 @@
             pltpu.VMEM((n_req, SLOTS, BLK), BF),
             pltpu.VMEM((n_req, SLOTS, BLK), BF),
             pltpu.VMEM((n_hid, rows, BLK), BF),
-            dma((2,)),
+            dma((4,)),
             dma((4, 15)),
             dma((4, 15)),
             req_sem,

time: 116 us -> 113 us (0.974)
  Pallas kernels: 113 us -> 110 us
    pallas_call x1, Pallas kernels: 113 us -> 110 us  [on_device(): pl.pallas_call(functools.partial(moe_kernel, n_req, n_hid), out_shape=jax...]
where the time goes in v4:
time: 113 us; the launch traced here: 112 us
  Pallas kernels  110 us (97%)
  local copies, waits for them, and re-layouts  1.76 us (2%)
    pallas_call x1, Pallas kernels, on_device(): pl.pallas_call(functools.partial(moe_kernel, n_req, n_hid), out_shape=jax...  110 us

profile of v4, /device:TPU:1, one launch (start us, length us, event | category | flops | bytes accessed | tf_op | source)
XLA Modules:
  0.0 111.7 jit_solution(11551124881521952736)
XLA Ops:
  0.0 110.0 %moe_block.1 = bf16[64,2880]{1,0:T(8,128)(2,1)} custom-call(bf16[64,2880]{1,0:T(8,128)(2,1)} %bitcast.10, bf16[64,2880]{1,0:T(8,128)(2,1)} %resid_hbm.1, bf16[2880]{0:T(1024)(128)(2,1)} %gain_ref.1, bf16[32,2880]{1,0:T(8,128)(2,1)} %bitcast.11, f32[1,32]{1,0:T(1,128)} %bitcast.13, s32[4,64]{1,0:T(4,128)} %bitcast.12, bf16[1,360]{1,0:T(2,128)(2,1)} %bgu_ref.1, ...), custom_call_target="tpu_custom_call" | custom-call | tf_op jit(solution)/shard_map/moe_block/pallas_call | solution.py:572
  110.0 1.8 %copy.12 = bf16[64,2880]{1,0:T(8,128)(2,1)} copy(bf16[64,2880]{1,0:T(8,128)(2,1)} %moe_block.1) | data formatting | bytes 737280

commit v5 on v4

--- a/solution.py
+++ b/solution.py
@@ -166,7 +166,10 @@
         b = lax.rem((y if c == 0 else x) + db, side)
         return a * side + b if c == 0 else b * side + a
 
-    def scatter_first(src, bufs, sems, make):
+    def order(n, q):
+        return (q // 2, q % 2) if n == 4 else (q, q)
+
+    def scatter_first(n, src, bufs, sems, make):
         rb1 = bufs[2]
         rb2 = bufs[3]
 
@@ -177,8 +180,8 @@
         def _(j):
             for c in range(2):
                 make(at(c, j, 2), c)
-            for q in range(4):
-                c, odd = q // 2, q % 2
+            for q in range(n):
+                c, odd = order(n, q)
                 peer = at(c, 0, 1) if odd else at(c, 0, 3)
                 send(q, j, src(at(c, j, 2), q), rb1.at[q, j], peer)
 
@@ -187,12 +190,12 @@
             for c in range(2):
                 make(at(c, j, 1), c)
                 make(at(c, j, 3), c)
-            for q in range(4):
-                c, odd = q // 2, q % 2
+            for q in range(n):
+                c, odd = order(n, q)
                 to = 3 if odd else 1
                 send(q, 4 + j, src(at(c, j, to), q), rb2.at[q, j, 0], at(c, 0, to))
 
-    def scatter_rest(src, bufs, sems, make):
+    def scatter_rest(n, src, bufs, sems, make):
         mid, sums, rb1, rb2, ra1, ra2 = bufs
 
         def send(q, k, ref, dst, peer):
@@ -203,8 +206,8 @@
 
         @pl.loop(0, 4)
         def _(j):
-            for q in range(4):
-                c, odd = q // 2, q % 2
+            for q in range(n):
+                c, odd = order(n, q)
                 to = 1 if odd else 3
                 landed(q, j, rb1.at[q, j])
                 both = src(at(c, j, to), q)[...].astype(F32) + rb1[q, j].astype(F32)
@@ -216,20 +219,20 @@
         def line_sum(j, q):
             landed(q, 4 + j, rb2.at[q, j, 0])
             landed(q, 8 + j, rb2.at[q, j, 1])
-            three = src(at(q // 2, j, 0), q)[...].astype(F32)
+            three = src(at(order(n, q)[0], j, 0), q)[...].astype(F32)
             return three + rb2[q, j, 0].astype(F32) + rb2[q, j, 1].astype(F32)
 
-        for q in range(4):
-            c, odd = q // 2, q % 2
+        for q in range(n):
+            c, odd = order(n, q)
             sums[q, 2] = line_sum(2, q).astype(BF)
             send(q, 12, sums.at[q, 2], ra1.at[q], at(c, 1 if odd else 3, 0))
-        for q in range(4):
-            c, odd = q // 2, q % 2
+        for q in range(n):
+            c, odd = order(n, q)
             to = 3 if odd else 1
             sums[q, to] = line_sum(to, q).astype(BF)
             send(q, 13, sums.at[q, to], ra2.at[q, 0], at(c, to, 0))
-        for q in range(4):
-            c, odd = q // 2, q % 2
+        for q in range(n):
+            c, odd = order(n, q)
             to = 1 if odd else 3
             near = line_sum(to, q)
             landed(q, 12, ra1.at[q])
@@ -244,7 +247,7 @@
 
         return result
 
-    def gather_over_hid(piece, sems, ready, after):
+    def gather_over_hid(n, piece, sems, ready, after):
         def ship(q, k, p, peer):
             ref = piece(p, q)
             hid_copy(ref, ref, sems[0].at[q, k], sems[1].at[p, q], peer).start()
@@ -253,8 +256,8 @@
             ref = piece(p, q)
             hid_copy(ref, ref, sems[0].at[q, 0], sems[1].at[p, q], p).wait_recv()
 
-        for q in range(4):
-            c = q // 2
+        for q in range(n):
+            c, _odd = order(n, q)
             ready(q)
             ship(q, 0, h, at(c, 1, 0))
             ship(q, 1, h, at(c, 3, 0))
@@ -262,8 +265,8 @@
             ship(q, 4, h, at(c, 0, 3))
         for c in range(2):
             after(h, c)
-        for q in range(4):
-            c, odd = q // 2, q % 2
+        for q in range(n):
+            c, odd = order(n, q)
             arrive(q, at(c, 1, 0))
             arrive(q, at(c, 3, 0))
             if odd:
@@ -279,8 +282,8 @@
             def _(i):
                 after(at(c, 2 * i + 1, 0), c)
 
-        for q in range(4):
-            c = q // 2
+        for q in range(n):
+            c, _odd = order(n, q)
             arrive(q, at(c, 2, 0))
             ship(q, 7, at(c, 2, 0), at(c, 0, 1))
             ship(q, 8, at(c, 2, 0), at(c, 0, 3))
@@ -288,8 +291,8 @@
         @pl.loop(0, 4)
         def _(i):
             j = lax.rem(i + i + i, 4)
-            for q in range(4):
-                c, odd = q // 2, q % 2
+            for q in range(n):
+                c, odd = order(n, q)
                 arrive(q, at(c, j, 1))
                 arrive(q, at(c, j, 3))
                 if odd:
@@ -308,13 +311,13 @@
         @pl.loop(0, 4)
         def _(i):
             j = lax.rem(i + i + i, 4)
-            for q in range(4):
-                arrive(q, at(q // 2, j, 2))
+            for q in range(n):
+                arrive(q, at(order(n, q)[0], j, 2))
             for c in range(2):
                 after(at(c, j, 2), c)
 
-    def sent(refs, sems):
-        for q in range(4):
+    def sent(n, refs, sems):
+        for q in range(n):
 
             @pl.loop(0, 15)
             def _(k):
@@ -325,12 +328,12 @@
         pass
 
     bufs1 = (mid1, sum1, rb1_1, rb2_1, ra1_1, ra2_1)
-    rowq1 = rows // 4
+    rowq1 = rows // 2
 
     def share(p, q):
         return attn_s.at[pl.ds(q * rowq1, rowq1), lanes(lax.rem(p, NBLK))]
 
-    scatter_first(share, bufs1, (s1, q1), nothing)
+    scatter_first(2, share, bufs1, (s1, q1), nothing)
 
     wr_s[...] = jnp.zeros(wr_s.shape, BF)
     wr_s[0:experts, 0:width] = wr_ref[...]
@@ -355,8 +358,8 @@
     chosen = dot_nt(same, chosen_t)
     mask = dot_nt(same, mask_t)
 
-    result1 = scatter_rest(share, bufs1, (s1, q1), nothing)
-    attention = jnp.concatenate([result1(q) for q in range(4)], axis=0)
+    result1 = scatter_rest(2, share, bufs1, (s1, q1), nothing)
+    attention = jnp.concatenate([result1(q) for q in range(2)], axis=0)
     stream = (resid_s[:, lanes(f)].astype(F32) + attention).astype(BF)
     stream_wide = stream.astype(F32)
 
@@ -437,9 +440,9 @@
             def _():
                 req_copy(zout.at[p], ag.at[h, p], s2.at[p], q2.at[p], p).wait_recv()
 
-    sent(lambda q: share(h, q), (s1, q1))
+    sent(2, lambda q: share(h, q), (s1, q1))
     ag[h, g] = zout[g]
-    gather_over_hid(piece, (s4, q4), arrived, use_half)
+    gather_over_hid(4, piece, (s4, q4), arrived, use_half)
 
     for side_at in range(2):
         mean = jnp.sum(ssq[side_at], axis=1, keepdims=True) * (1.0 / width)
@@ -462,7 +465,7 @@
         return pout.at[p, pl.ds(q * rowq, rowq)]
 
     bufs5 = (mid5, sum5, rb1, rb2, ra1, ra2)
-    scatter_first(part, bufs5, (s5, q5), down)
+    scatter_first(4, part, bufs5, (s5, q5), down)
     total_stats = stat_s[...]
     for d in range(1, NBLK):
         pf = lax.rem(f - d + NBLK, NBLK)
@@ -476,7 +479,7 @@
     combine_wide = dot_nt(combine, expand_t)
     weights = jnp.where(chosen > 0.5, combine_wide, 0.0).astype(BF)
 
-    result5 = scatter_rest(part, bufs5, (s5, q5), down)
+    result5 = scatter_rest(4, part, bufs5, (s5, q5), down)
 
     for q in range(4):
         expert_out = result5(q) + db_s[:, lanes(f)]
@@ -490,8 +493,8 @@
 
     zbin[g] = zbout[g]
 
-    sent(lambda q: piece(h, q), (s4, q4))
-    sent(lambda q: part(h, q), (s5, q5))
+    sent(4, lambda q: piece(h, q), (s4, q4))
+    sent(4, lambda q: part(h, q), (s5, q5))
 
     @pl.loop(1, NBLK)
     def _(d):
@@ -528,24 +531,24 @@
             p = lax.rem(g + d, n_req)
             req_copy(zbout.at[p], zbin.at[p], s6.at[p], q6.at[p], p).wait_send()
 
-    gather_over_hid(final, (s7, q7), lambda q: None, wait_back)
+    gather_over_hid(2, final, (s7, q7), lambda q: None, wait_back)
 
     for b in range(NBLK):
         size = min(BLK, width - b * BLK)
         both = rfin[b].astype(F32) + rfin[NBLK + b].astype(F32)
         out_ref[:, b * BLK : b * BLK + size] = both[:, :size].astype(BF)
 
-    sent(lambda q: final(h, q), (s7, q7))
-
-
-def ring_buffers(size):
+    sent(2, lambda q: final(h, q), (s7, q7))
+
+
+def ring_buffers(n, size):
     return [
-        pltpu.VMEM((4, 4, size, BLK), BF),
-        pltpu.VMEM((4, 4, size, BLK), BF),
-        pltpu.VMEM((4, 4, size, BLK), BF),
-        pltpu.VMEM((4, 4, 2, size, BLK), BF),
-        pltpu.VMEM((4, size, BLK), BF),
-        pltpu.VMEM((4, 2, size, BLK), BF),
+        pltpu.VMEM((n, 4, size, BLK), BF),
+        pltpu.VMEM((n, 4, size, BLK), BF),
+        pltpu.VMEM((n, 4, size, BLK), BF),
+        pltpu.VMEM((n, 4, 2, size, BLK), BF),
+        pltpu.VMEM((n, size, BLK), BF),
+        pltpu.VMEM((n, 2, size, BLK), BF),
     ]
 
 
@@ -586,7 +589,7 @@
             pltpu.VMEM(down_weight.shape[1:], BF),
             pltpu.VMEM((512, wide), BF),
             pltpu.VMEM((256, wide), BF),
-            *ring_buffers(rows // 4),
+            *ring_buffers(2, rows // 2),
             pltpu.VMEM((rows, 128), F32),
             pltpu.VMEM((NBLK, rows, 128), F32),
             pltpu.VMEM((n_req, SLOTS, BLK), BF),
@@ -595,7 +598,7 @@
             pltpu.VMEM((2, per, 128), F32),
             pltpu.VMEM((2, per, 256), BF),
             pltpu.VMEM((n_hid, per, BLK), BF),
-            *ring_buffers(per // 4),
+            *ring_buffers(4, per // 4),
             pltpu.VMEM((n_req, SLOTS, BLK), BF),
             pltpu.VMEM((n_req, SLOTS, BLK), BF),
             pltpu.VMEM((n_hid, rows, BLK), BF),

time: 113 us -> 114 us (level)
  no operation moved by 1% of the time
where the time goes in v5:
time: 114 us; the launch traced here: 112 us
  Pallas kernels  110 us (96%)
  local copies, waits for them, and re-layouts  1.76 us (2%)
    pallas_call x1, Pallas kernels, on_device(): pl.pallas_call(functools.partial(moe_kernel, n_req, n_hid), out_shape=jax...  110 us

profile of v5, /device:TPU:1, one launch (start us, length us, event | category | flops | bytes accessed | tf_op | source)
XLA Modules:
  0.0 112.0 jit_solution(4008695952324365047)
XLA Ops:
  0.0 110.3 %moe_block.1 = bf16[64,2880]{1,0:T(8,128)(2,1)} custom-call(bf16[64,2880]{1,0:T(8,128)(2,1)} %bitcast.10, bf16[64,2880]{1,0:T(8,128)(2,1)} %resid_hbm.1, bf16[2880]{0:T(1024)(128)(2,1)} %gain_ref.1, bf16[32,2880]{1,0:T(8,128)(2,1)} %bitcast.11, f32[1,32]{1,0:T(1,128)} %bitcast.13, s32[4,64]{1,0:T(4,128)} %bitcast.12, bf16[1,360]{1,0:T(2,128)(2,1)} %bgu_ref.1, ...), custom_call_target="tpu_custom_call" | custom-call | tf_op jit(solution)/shard_map/moe_block/pallas_call | solution.py:575
  110.3 1.8 %copy.12 = bf16[64,2880]{1,0:T(8,128)(2,1)} copy(bf16[64,2880]{1,0:T(8,128)(2,1)} %moe_block.1) | data formatting | bytes 737280
